TPU v7x, 512 devices: a whole 4x4x16 slice. The times are simulated.
512 devices in a mesh: blk: 64 (over y, z_lo, core), grp: 8 (over z_hi, x).
Axes of the slice: x: 4, y: 4, z: 16 (z_hi: 2, z_lo: 8; z = z_hi * 8 + z_lo), core: 2. Of those that a mesh axis runs over, the one named last changes fastest.
Arguments:
- occupied: bfloat16 [32768, 1024], P('blk'), may hold values from -6 to 6
- integrals: bfloat16 [64, 8, 3, 64, 4096], P('blk', 'grp'), may hold values from -0.75 to 0.75
- metric_inv: bfloat16 [65536, 1024], P('blk')
- pattern: int32 [64, 8, 3, 4], P('blk', 'grp'), may hold values from 0 to 63, as said below
- support: int32 [64, 8], P('blk'), may hold values from 0 to 1023, as said below
Outputs:
- exchange: float32 [32768, 512], P(('blk', 'grp'))
Inputs may be any that keep to these rules, and one draw needn't show every extreme that they name: Field 0 of every slot of pattern[r, g] is a region within distance 3 of r along the closed chain of 64 regions; field 1 is below 8; field 2 is below 16; field 3 is 1 on a leading run of slots and 0 after it, and in every draw some basis block has all 3 slots live. `support`: the 8 orbitals of one region are distinct.
All inputs are finite; a program needn't handle non-finite values.
Results may differ from a plain program's by a relative error of at most 0.0045.
Values may be sent and summed in bfloat16 or wider, within the bound.
No kernel may reach another device: no remote copies, remote signals or barrier semaphores. Data moves between devices by JAX's collectives and lax.ppermute only.
A program may use at most 64 MiB of HBM per device.

v0:
```python
import jax
import jax.numpy as jnp
from jax import lax
from jax.experimental import pallas as pl
from jax.experimental.pallas import tpu as pltpu
from jax.sharding import PartitionSpec as P


BF = 64
AB = 64
AUXR = 1024
OSUP = 8
NT = 3
REACH = 3
XN = 4
DATA = OSUP * BF * NT * AB // 128
ROWS = DATA + 16
F32 = jnp.float32
BF16 = jnp.bfloat16


def near(region, group, offset, regions, zlo):
    target = region + offset
    step = target // 2 - region // 2
    z = (group // XN) * zlo + (region // 2) % zlo
    z = (z + step) % (2 * zlo)
    return (target % regions) * (2 * XN) + (z // zlo) * XN + group % XN


def partner_offset(region, x, j):
    distance, phase = ((1, 0), (1, 1), (2, 0), (2, 1))[x] if j == 0 else ((3, 0), (3, 1), (0, 0), (0, 1))[x]
    place = (region // 2) if distance == 2 else region
    return distance if (place + phase) % 2 == 0 else -distance


def request_pairs(j, regions):
    zlo = 8
    return [
        (r * 8 + g, near(r, g, partner_offset(r, g % XN, j), regions, zlo))
        for r in range(regions)
        for g in range(2 * XN)
    ]


def contribution_kernel(region_ref, pattern_ref, window_ref, integrals_ref, out_ref, sa_ref, sb_ref):
    region = region_ref[0]
    a = [pattern_ref[0, 0, t, 2] for t in range(NT)]
    live = [pattern_ref[0, 0, t, 3] for t in range(NT)]
    lane8 = lax.broadcasted_iota(jnp.int32, (OSUP, 128), 1)
    low8 = lane8 < 64

    def tile(t, want_high):
        offset = (pattern_ref[0, 0, t, 0] - region + 64 + REACH) % 64 - REACH
        distance = jnp.abs(offset)
        place = jnp.where(distance == 2, region // 2, region)
        phase = jnp.where(offset > 0, place % 2, 1 - place % 2)
        x = jnp.where(distance == 2, 2, 0) + phase
        x = jnp.where(distance == 0, 2, x)
        j = jnp.where(distance == 1, 0, jnp.where(distance == 2, 0, 1))
        m = pattern_ref[0, 0, t, 1]
        part = window_ref[x, j, :, pl.ds(pl.multiple_of((m // 2) * 128, 128), 128)].astype(F32)
        return pltpu.roll(part, 64 * ((m % 2) ^ want_high), 1)

    chunk0 = jnp.where(low8, tile(0, 0), tile(1, 1))
    chunk1 = tile(2, 0)[:, :64]
    rep = [jnp.int32(0)]
    rep.append(jnp.where(a[1] == a[0], 0, 1))
    rep.append(jnp.where(a[2] == a[0], 0, jnp.where(a[2] == a[1], 1, 2)))
    rows = []
    for t in range(NT):
        w = [jnp.where(rep[u] == t, live[u], 0).astype(F32) for u in range(NT)]
        first = chunk0 * jnp.where(low8, w[0], w[1])
        rows.append(jnp.concatenate([first, chunk1 * w[2]], axis=1))
    lhs = jnp.concatenate(rows, axis=0).astype(BF16)
    tiles = integrals_ref[0, 0].reshape(NT * BF, BF * AB)
    c = jnp.dot(lhs, tiles, preferred_element_type=F32)
    for k in range(BF * AB // 128):
        v = [c[t * 8 : (t + 1) * 8, k * 128 : (k + 1) * 128] for t in range(NT)]
        s0, s1, s2 = [pltpu.roll(u, 64, 1) for u in v]
        half = pltpu.roll(v[2], 4, 0)
        half_s = pltpu.roll(s2, 4, 0)
        sa_ref[pl.ds(2 * k, OSUP, stride=BF), :] = jnp.where(low8, v[0], s1)
        sa_ref[pl.ds(2 * k + 1, OSUP, stride=BF), :] = jnp.where(low8, s0, v[1])
        sb_ref[pl.ds(2 * k, OSUP // 2, stride=BF), :] = jnp.where(low8, v[2], half_s)[: OSUP // 2]
        sb_ref[pl.ds(2 * k + 1, OSUP // 2, stride=BF), :] = jnp.where(low8, s2, half)[: OSUP // 2]
    out_ref[0:512, :] = sa_ref[...].astype(BF16)
    out_ref[512:768, :] = sb_ref[...].astype(BF16)
    lane = lax.broadcasted_iota(jnp.int32, (16, 128), 1)
    tag = jnp.where(lane == 0, a[0], jnp.where(lane == 1, a[1], a[2]))
    out_ref[768:784, :] = tag.astype(F32).astype(BF16)


def blocks_of(tag_row):
    row = tag_row.astype(F32)
    lane = lax.broadcasted_iota(jnp.int32, row.shape, 1)
    return [jnp.sum(jnp.where(lane == t, row, 0.0)).astype(jnp.int32) for t in range(NT)]


def weights_of(metric_ref, rows, cols):
    low = lax.broadcasted_iota(jnp.int32, (AB, 128), 1) < 64
    zero = jnp.zeros((AB, 128), F32)

    def piece(p, q, want_high):
        part = metric_ref[p, :, pl.ds(pl.multiple_of((q // 2) * 128, 128), 128)].astype(F32)
        return pltpu.roll(part, 64 * ((q % 2) ^ want_high), 1)

    lo, hi = [], []
    for p in rows:
        first = jnp.where(low, piece(p, cols[0], 0), piece(p, cols[1], 1))
        second = piece(p, cols[2], 0)
        lo.append(jnp.concatenate([first, jnp.where(low, second, zero)], axis=1))
        hi.append(jnp.concatenate([first, jnp.where(low, zero, pltpu.roll(second, 64, 1))], axis=1))
    blank = jnp.zeros((AB, 256), F32)
    lo = jnp.concatenate(lo + [blank], axis=0).astype(BF16)
    hi = jnp.concatenate(hi[:2] + [blank, hi[2]], axis=0).astype(BF16)
    return lo, hi


def halves(a_part, b_part):
    lo = jnp.concatenate([a_part[0:256], b_part], axis=1)
    hi = jnp.concatenate([a_part[256:512], b_part], axis=1)
    return lo, hi


def by_orbital(lo, hi):
    parts = [lo[i * 64 : (i + 1) * 64] for i in range(4)] + [hi[i * 64 : (i + 1) * 64] for i in range(4)]
    return jnp.concatenate(parts, axis=1)


def fitted_of(lo, hi, wlo, whi):
    flo = jnp.dot(lo, wlo, preferred_element_type=F32).astype(BF16)
    fhi = jnp.dot(hi, whi, preferred_element_type=F32).astype(BF16)
    return by_orbital(flo, fhi)


NT_DIMS = (((1,), (1,)), ((), ()))


def early_kernel(own_ref, all_ref, metric_ref, out_ref):
    cols = blocks_of(own_ref[768:784, :][0:1])
    own = by_orbital(*halves(own_ref[0:512, :], own_ref[512:768, :]))
    fitted = []
    for x in range(XN):
        rows = blocks_of(all_ref[x, 768:784, :][0:1])
        wlo, whi = weights_of(metric_ref, rows, cols)
        lo, hi = halves(all_ref[x, 0:512, :], all_ref[x, 512:768, :])
        fitted.append(fitted_of(lo, hi, wlo, whi))
    fitted = jnp.concatenate(fitted, axis=0)
    out_ref[...] = lax.dot_general(own, fitted, NT_DIMS, preferred_element_type=F32)


def late_kernel(far_ref, all_ref, metric_ref, out_ref):
    rows = blocks_of(far_ref[768:784, :][0:1])
    lo, hi = halves(far_ref[0:512, :], far_ref[512:768, :])
    for x in range(XN):
        cols = blocks_of(all_ref[x, 768:784, :][0:1])
        wlo, whi = weights_of(metric_ref, rows, cols)
        fitted = fitted_of(lo, hi, wlo, whi)
        mine = by_orbital(*halves(all_ref[x, 0:512, :], all_ref[x, 512:768, :]))
        block = lax.dot_general(mine, fitted, NT_DIMS, preferred_element_type=F32)
        out_ref[x] = jnp.concatenate([block[0:32], block[32:64]], axis=1)


def join_kernel(group_ref, early_ref, late_ref, out_ref):
    high = group_ref[0] >= XN
    late = jnp.concatenate(
        [
            jnp.concatenate([late_ref[x][:, 0:64] for x in range(XN)], axis=1),
            jnp.concatenate([late_ref[x][:, 64:128] for x in range(XN)], axis=1),
        ],
        axis=0,
    )
    early = early_ref[...]
    out_ref[:, 0:256] = jnp.where(high, late, early)
    out_ref[:, 256:512] = jnp.where(high, early, late)


def smem():
    return pl.BlockSpec(memory_space=pltpu.SMEM)


def vmem():
    return pl.BlockSpec(memory_space=pltpu.VMEM)


def in_vmem(value):
    return pltpu.with_memory_space_constraint(value, pltpu.VMEM)


def per_device(occupied, integrals, metric_inv, pattern, support):
    regions = lax.axis_size("blk")
    axes = ("blk", "grp")
    groups = [list(range(XN)), list(range(XN, 2 * XN))]
    region = lax.axis_index("blk").astype(jnp.int32).reshape(1)
    group = lax.axis_index("grp").astype(jnp.int32).reshape(1)

    def spread(value):
        value = jnp.broadcast_to(value[None], (XN,) + value.shape)
        return lax.all_to_all(value, "grp", 0, 0, axis_index_groups=groups)

    pairs = [request_pairs(j, regions) for j in range(2)]
    asked = [lax.ppermute(support, axes, pairs[j]) for j in range(2)]
    asked = jnp.concatenate(asked, axis=1)[0]
    pick = (asked[:, None] == jnp.arange(occupied.shape[1], dtype=jnp.int32)[None, :]).astype(BF16)
    selected = lax.dot_general(pick, occupied, NT_DIMS, preferred_element_type=F32).astype(BF16)
    back = [[(d, s) for s, d in p] for p in pairs]
    got = [lax.ppermute(selected[j * OSUP : (j + 1) * OSUP], axes, back[j]) for j in range(2)]
    window = spread(jnp.stack(got, 0))

    message = pl.pallas_call(
        contribution_kernel,
        out_shape=jax.ShapeDtypeStruct((ROWS, 128), BF16),
        in_specs=[smem(), smem(), vmem(), vmem()],
        out_specs=vmem(),
        scratch_shapes=[pltpu.VMEM((512, 128), F32), pltpu.VMEM((256, 128), F32)],
        name="contribution",
    )(region, pattern, in_vmem(window), integrals)

    far = lax.ppermute(message, "grp", [(g, (g + XN) % (2 * XN)) for g in range(2 * XN)])
    everyone = spread(message)
    metric = metric_inv.reshape(AUXR // AB, AB, AUXR)
    early = pl.pallas_call(
        early_kernel,
        out_shape=jax.ShapeDtypeStruct((BF, XN * BF), F32),
        in_specs=[vmem(), vmem(), vmem()],
        out_specs=vmem(),
        name="early",
    )(message, in_vmem(everyone), metric)
    late = pl.pallas_call(
        late_kernel,
        out_shape=jax.ShapeDtypeStruct((XN, BF // 2, 2 * BF), F32),
        in_specs=[vmem(), vmem(), vmem()],
        out_specs=vmem(),
        name="late",
    )(in_vmem(far), in_vmem(everyone), metric)
    late = lax.all_to_all(late, "grp", 0, 0, axis_index_groups=groups)
    return pl.pallas_call(
        join_kernel,
        out_shape=jax.ShapeDtypeStruct((BF, 2 * XN * BF), F32),
        in_specs=[smem(), vmem(), vmem()],
        out_specs=vmem(),
        name="join",
    )(group, early, in_vmem(late))


def solution(mesh):
    placed = (
        P("blk", None),
        P("blk", "grp", None, None, None),
        P("blk", None),
        P("blk", "grp", None, None),
        P("blk", None),
    )
    return jax.shard_map(
        per_device, mesh=mesh, in_specs=placed, out_specs=P(("blk", "grp"), None), check_vma=False
    )
```

profile of v0, /device:TPU:1, one launch (start us, length us, event | category | flops | bytes accessed | tf_op | source)
XLA Modules:
  0.0 89.5 jit_solution(2197489082210344082)
XLA Ops:
  0.0 8.9 %collective-permute-start = (s32[1,8]{1,0:T(1,128)}, s32[1,8]{1,0:T(1,128)S(1)}, u32[]{:S(2)}, u32[]{:S(2)}) collective-permute-start(s32[1,8]{1,0:T(1,128)} %param.9), channel_id=1, source_target_pairs={{0,8},{1,509},{2,18},{3,503},{4,12},{5,505},{6,22},{7,499},{8,0},{... | collective-permute-start | bytes 104 | tf_op jit(solution)/shard_map/ppermute | solution.py:202
  8.9 8.1 %collective-permute-start.1 = (s32[1,8]{1,0:T(1,128)}, s32[1,8]{1,0:T(1,128)S(1)}, u32[]{:S(2)}, u32[]{:S(2)}) collective-permute-start(s32[1,8]{1,0:T(1,128)} %param.9), channel_id=1, source_target_pairs={{0,24},{1,493},{2,2},{3,3},{4,28},{5,489},{6,6},{7,7},{8,500},{9,3... | collective-permute-start | bytes 104 | tf_op jit(solution)/shard_map/ppermute | solution.py:202
  17.0 0.0 collective-permute-done
  17.0 1.4 %collective-permute-done.1 = s32[1,8]{1,0:T(1,128)S(1)} collective-permute-done((s32[1,8]{1,0:T(1,128)}, s32[1,8]{1,0:T(1,128)S(1)}, u32[]{:S(2)}, u32[]{:S(2)}) %collective-permute-start.1) | collective-permute-done | bytes 64 | tf_op jit(solution)/shard_map/ppermute | solution.py:202
  18.4 0.1 add_bitcast_fusion
  18.5 0.4 convolution_convert_fusion
  18.8 1.9 %collective-permute-start.2 = (bf16[8,512]{1,0:T(8,128)(2,1)S(1)}, bf16[8,512]{1,0:T(8,128)(2,1)S(1)}, u32[]{:S(2)}, u32[]{:S(2)}) collective-permute-start(bf16[8,512]{1,0:T(8,128)(2,1)S(1)} %get-tuple-element.5), channel_id=1, source_target_pairs={{8,0},{509,1},{18,2},{503,3},{12,4},{505,5},{22,6},{499,7},{0,8},{... | collective-permute-start | bytes 24584 | tf_op jit(solution)/shard_map/ppermute | solution.py:207
  20.8 7.0 %collective-permute-start.3 = (bf16[8,512]{1,0:T(8,128)(2,1)S(1)}, bf16[8,512]{1,0:T(8,128)(2,1)S(1)}, u32[]{:S(2)}, u32[]{:S(2)}) collective-permute-start(bf16[8,512]{1,0:T(8,128)(2,1)S(1)} %get-tuple-element.6), channel_id=1, source_target_pairs={{24,0},{493,1},{2,2},{3,3},{28,4},{489,5},{6,6},{7,7},{500,8},{33,... | collective-permute-start | bytes 24584 | tf_op jit(solution)/shard_map/ppermute | solution.py:207
  27.8 1.3 %collective-permute-done.3 = bf16[8,512]{1,0:T(8,128)(2,1)S(1)} collective-permute-done((bf16[8,512]{1,0:T(8,128)(2,1)S(1)}, bf16[8,512]{1,0:T(8,128)(2,1)S(1)}, u32[]{:S(2)}, u32[]{:S(2)}) %collective-permute-start.3) | collective-permute-done | bytes 8224 | tf_op jit(solution)/shard_map/ppermute | solution.py:207
  29.1 0.6 broadcast_in_dim.4
  29.7 3.3 %all-to-all-start = ((bf16[4,2,8,512]{3,2,1,0:T(8,128)(2,1)}), bf16[4,2,8,512]{3,2,1,0:T(8,128)(2,1)S(1)}, u32[]{:S(2)}, u32[]{:S(2)}) async-start(bf16[4,2,8,512]{3,2,1,0:T(8,128)(2,1)} %broadcast_in_dim.4), calls=%async_computation | async-start | bytes 131072 | tf_op jit(solution)/shard_map/all_to_all | solution.py:199
  33.0 1.2 %copy.6.pattern_ref = s32[1,1,3,4]{3,2,1,0:T(4,128)} copy(s32[1,1,3,4]{3,1,2,0:T(1,128)} %param.8) | data formatting | bytes 96 | tf_op args[3]
  34.3 3.2 %all-to-all-done.window_ref = bf16[4,2,8,512]{3,2,1,0:T(8,128)(2,1)S(1)} async-done(((bf16[4,2,8,512]{3,2,1,0:T(8,128)(2,1)}), bf16[4,2,8,512]{3,2,1,0:T(8,128)(2,1)S(1)}, u32[]{:S(2)}, u32[]{:S(2)}) %all-to-all-start) | async-done | bytes 65568 | tf_op jit(solution)/shard_map/all_to_all | solution.py:199
  37.4 2.8 %contribution.1.own_ref = bf16[784,128]{1,0:T(8,128)(2,1)} custom-call(s32[1]{0:T(128)} %bitcast.1.region_ref, s32[1,1,3,4]{3,2,1,0:T(4,128)} %copy.6.pattern_ref, bf16[4,2,8,512]{3,2,1,0:T(8,128)(2,1)S(1)} %all-to-all-done.window_ref, bf16[1,1,3,64,4096]{4,3,2,1,0:T(8,128)(2,1)} %integrals_ref.1), custom_call_target="tpu_custom_call" | custom-call | tf_op jit(solution)/shard_map/contribution/pallas_call | solution.py:210
  40.2 2.0 %broadcast_in_dim.5 = bf16[4,784,128]{2,1,0:T(8,128)(2,1)} broadcast(bf16[784,128]{1,0:T(8,128)(2,1)} %contribution.1.own_ref), dimensions={1,2} | broadcast | bytes 1003520 | tf_op jit(solution)/shard_map/broadcast_in_dim | solution.py:198
  42.2 3.5 %all-to-all-start.1 = ((bf16[4,784,128]{2,1,0:T(8,128)(2,1)}), bf16[4,784,128]{2,1,0:T(8,128)(2,1)S(1)}, u32[]{:S(2)}, u32[]{:S(2)}) async-start(bf16[4,784,128]{2,1,0:T(8,128)(2,1)} %broadcast_in_dim.5), calls=%async_computation.1 | async-start | bytes 1605632 | tf_op jit(solution)/shard_map/all_to_all | solution.py:199
  45.7 8.9 %collective-permute-start.4 = (bf16[784,128]{1,0:T(8,128)(2,1)S(1)}, bf16[784,128]{1,0:T(8,128)(2,1)S(1)}, u32[]{:S(2)}, u32[]{:S(2)}) collective-permute-start(bf16[784,128]{1,0:T(8,128)(2,1)S(1)} %copy-done.1), channel_id=1, source_target_pairs={{0,4},{1,5},{2,6},{3,7},{4,0},{5,1},{6,2},{7,3},{8,12},{9,13},{10,... | collective-permute-start | bytes 602120 | tf_op jit(solution)/shard_map/ppermute | solution.py:219
  54.7 21.0 %collective-permute-done.4.far_ref = bf16[784,128]{1,0:T(8,128)(2,1)S(1)} collective-permute-done((bf16[784,128]{1,0:T(8,128)(2,1)S(1)}, bf16[784,128]{1,0:T(8,128)(2,1)S(1)}, u32[]{:S(2)}, u32[]{:S(2)}) %collective-permute-start.4) | collective-permute-done | bytes 200736 | tf_op jit(solution)/shard_map/ppermute | solution.py:219
  75.7 0.0 all-to-all-done.1.all_ref
  75.7 3.5 %late.1 = f32[4,32,128]{2,1,0:T(8,128)} custom-call(bf16[784,128]{1,0:T(8,128)(2,1)S(1)} %collective-permute-done.4.far_ref, bf16[4,784,128]{2,1,0:T(8,128)(2,1)S(1)} %all-to-all-done.1.all_ref, bf16[16,64,1024]{2,1,0:T(8,128)(2,1)} %bitcast.8), custom_call_target="tpu_custom_call" | custom-call | tf_op jit(solution)/shard_map/late/pallas_call | solution.py:229
  79.3 4.2 %all-to-all-start.2 = ((f32[4,32,128]{2,1,0:T(8,128)}), f32[4,32,128]{2,1,0:T(8,128)S(1)}, u32[]{:S(2)}, u32[]{:S(2)}) async-start(f32[4,32,128]{2,1,0:T(8,128)} %late.1), calls=%async_computation.2 | async-start | bytes 131072 | tf_op jit(solution)/shard_map/all_to_all | solution.py:236
  83.4 3.8 %early.1.early_ref = f32[64,256]{1,0:T(8,128)} custom-call(bf16[784,128]{1,0:T(8,128)(2,1)} %contribution.1.own_ref, bf16[4,784,128]{2,1,0:T(8,128)(2,1)S(1)} %all-to-all-done.1.all_ref, bf16[16,64,1024]{2,1,0:T(8,128)(2,1)} %bitcast.9), custom_call_target="tpu_custom_call" | custom-call | tf_op jit(solution)/shard_map/early/pallas_call | solution.py:222
  87.2 0.7 all-to-all-done.2.late_ref
  87.9 1.6 %join.1 = f32[64,512]{1,0:T(8,128)} custom-call(s32[1]{0:T(128)} %bitcast.group_ref, f32[64,256]{1,0:T(8,128)} %early.1.early_ref, f32[4,32,128]{2,1,0:T(8,128)S(1)} %all-to-all-done.2.late_ref), custom_call_target="tpu_custom_call" | custom-call | tf_op jit(solution)/shard_map/join/pallas_call | solution.py:237
  (7 shorter events, 0.0 us)
Async XLA Ops:
  0.0 18.5 %copy-start = (bf16[512,1024]{1,0:T(8,128)(2,1)S(1)}, bf16[512,1024]{1,0:T(8,128)(2,1)}, u32[]{:S(2)}) copy-start(bf16[512,1024]{1,0:T(8,128)(2,1)} %param.5) | copy-start | bytes 3145732
  0.0 17.0 %collective-permute-start = (s32[1,8]{1,0:T(1,128)}, s32[1,8]{1,0:T(1,128)S(1)}, u32[]{:S(2)}, u32[]{:S(2)}) collective-permute-start(s32[1,8]{1,0:T(1,128)} %param.9), channel_id=1, source_target_pairs={{0,8},{1,509},{2,18},{3,503},{4,12},{5,505},{6,22},{7,499},{8,0},{... | collective-permute-start | bytes 104 | tf_op jit(solution)/shard_map/ppermute | solution.py:202
  8.9 9.5 %collective-permute-start.1 = (s32[1,8]{1,0:T(1,128)}, s32[1,8]{1,0:T(1,128)S(1)}, u32[]{:S(2)}, u32[]{:S(2)}) collective-permute-start(s32[1,8]{1,0:T(1,128)} %param.9), channel_id=1, source_target_pairs={{0,24},{1,493},{2,2},{3,3},{4,28},{5,489},{6,6},{7,7},{8,500},{9,3... | collective-permute-start | bytes 104 | tf_op jit(solution)/shard_map/ppermute | solution.py:202
  18.8 8.9 %collective-permute-start.2 = (bf16[8,512]{1,0:T(8,128)(2,1)S(1)}, bf16[8,512]{1,0:T(8,128)(2,1)S(1)}, u32[]{:S(2)}, u32[]{:S(2)}) collective-permute-start(bf16[8,512]{1,0:T(8,128)(2,1)S(1)} %get-tuple-element.5), channel_id=1, source_target_pairs={{8,0},{509,1},{18,2},{503,3},{12,4},{505,5},{22,6},{499,7},{0,8},{... | collective-permute-start | bytes 24584 | tf_op jit(solution)/shard_map/ppermute | solution.py:207
  20.8 8.3 %collective-permute-start.3 = (bf16[8,512]{1,0:T(8,128)(2,1)S(1)}, bf16[8,512]{1,0:T(8,128)(2,1)S(1)}, u32[]{:S(2)}, u32[]{:S(2)}) collective-permute-start(bf16[8,512]{1,0:T(8,128)(2,1)S(1)} %get-tuple-element.6), channel_id=1, source_target_pairs={{24,0},{493,1},{2,2},{3,3},{28,4},{489,5},{6,6},{7,7},{500,8},{33,... | collective-permute-start | bytes 24584 | tf_op jit(solution)/shard_map/ppermute | solution.py:207
  29.7 7.7 %all-to-all-start = ((bf16[4,2,8,512]{3,2,1,0:T(8,128)(2,1)}), bf16[4,2,8,512]{3,2,1,0:T(8,128)(2,1)S(1)}, u32[]{:S(2)}, u32[]{:S(2)}) async-start(bf16[4,2,8,512]{3,2,1,0:T(8,128)(2,1)} %broadcast_in_dim.4), calls=%async_computation | async-start | bytes 131072 | tf_op jit(solution)/shard_map/all_to_all | solution.py:199
  40.2 5.5 %copy-start.1 = (bf16[784,128]{1,0:T(8,128)(2,1)S(1)}, bf16[784,128]{1,0:T(8,128)(2,1)}, u32[]{:S(2)}) copy-start(bf16[784,128]{1,0:T(8,128)(2,1)} %contribution.1.own_ref) | copy-start | bytes 602116
  42.2 33.5 %all-to-all-start.1 = ((bf16[4,784,128]{2,1,0:T(8,128)(2,1)}), bf16[4,784,128]{2,1,0:T(8,128)(2,1)S(1)}, u32[]{:S(2)}, u32[]{:S(2)}) async-start(bf16[4,784,128]{2,1,0:T(8,128)(2,1)} %broadcast_in_dim.5), calls=%async_computation.1 | async-start | bytes 1605632 | tf_op jit(solution)/shard_map/all_to_all | solution.py:199
  45.7 30.0 %collective-permute-start.4 = (bf16[784,128]{1,0:T(8,128)(2,1)S(1)}, bf16[784,128]{1,0:T(8,128)(2,1)S(1)}, u32[]{:S(2)}, u32[]{:S(2)}) collective-permute-start(bf16[784,128]{1,0:T(8,128)(2,1)S(1)} %copy-done.1), channel_id=1, source_target_pairs={{0,4},{1,5},{2,6},{3,7},{4,0},{5,1},{6,2},{7,3},{8,12},{9,13},{10,... | collective-permute-start | bytes 602120 | tf_op jit(solution)/shard_map/ppermute | solution.py:219
  79.3 8.7 %all-to-all-start.2 = ((f32[4,32,128]{2,1,0:T(8,128)}), f32[4,32,128]{2,1,0:T(8,128)S(1)}, u32[]{:S(2)}, u32[]{:S(2)}) async-start(f32[4,32,128]{2,1,0:T(8,128)} %late.1), calls=%async_computation.2 | async-start | bytes 131072 | tf_op jit(solution)/shard_map/all_to_all | solution.py:236
where the time goes:
time: 90.1 us; the launch traced here: 89.5 us
  starting transfers between devices  45.8 us (51%)
  waiting for transfers between devices  27.6 us (31%)
  Pallas kernels  11.7 us (13%)
  local copies, waits for them, and re-layouts  3.91 us (4%)
    ppermute x1, waiting for transfers between devices, per_device(): lax.ppermute(message, 'grp', [(g, (g + XN) % (2 * XN)) for g in range(2 *...  21 us
    ppermute x2, starting transfers between devices, per_device(): asked = [lax.ppermute(support, axes, pairs[j]) for j in range(2)]  17 us
    ppermute x1, starting transfers between devices, per_device(): lax.ppermute(message, 'grp', [(g, (g + XN) % (2 * XN)) for g in range(2 *...  8.93 us
    ppermute x2, starting transfers between devices, per_device(): lax.ppermute(selected[j * OSUP:(j + 1) * OSUP], axes, back[j])  8.89 us
    all_to_all x2, starting transfers between devices, spread(): return lax.all_to_all(value, 'grp', 0, 0, axis_index_groups=groups)  6.78 us
    all_to_all x1, starting transfers between devices, per_device(): late = lax.all_to_all(late, 'grp', 0, 0, axis_index_groups=groups)  4.18 us
    pallas_call x1, Pallas kernels, per_device(): pl.pallas_call(early_kernel, out_shape=jax.ShapeDtypeStruct((BF, XN * BF)...  3.81 us
    pallas_call x1, Pallas kernels, per_device(): pl.pallas_call(late_kernel, out_shape=jax.ShapeDtypeStruct((XN, BF // 2,...  3.53 us
  transfers between devices with their start and end apart: 8, of which 5 were waited for; matrix products, arithmetic and copies ran while one was open for 1% of the time, Pallas kernels for 4%

commit v1 on v0

--- a/solution.py
+++ b/solution.py
@@ -11,7 +11,6 @@
 AUXR = 1024
 OSUP = 8
 NT = 3
-REACH = 3
 XN = 4
 DATA = OSUP * BF * NT * AB // 128
 ROWS = DATA + 16
@@ -19,30 +18,25 @@
 BF16 = jnp.bfloat16
 
 
-def near(region, group, offset, regions, zlo):
-    target = region + offset
-    step = target // 2 - region // 2
-    z = (group // XN) * zlo + (region // 2) % zlo
-    z = (z + step) % (2 * zlo)
-    return (target % regions) * (2 * XN) + (z // zlo) * XN + group % XN
-
-
-def partner_offset(region, x, j):
-    distance, phase = ((1, 0), (1, 1), (2, 0), (2, 1))[x] if j == 0 else ((3, 0), (3, 1), (0, 0), (0, 1))[x]
-    place = (region // 2) if distance == 2 else region
-    return distance if (place + phase) % 2 == 0 else -distance
-
-
-def request_pairs(j, regions):
-    zlo = 8
-    return [
-        (r * 8 + g, near(r, g, partner_offset(r, g % XN, j), regions, zlo))
-        for r in range(regions)
-        for g in range(2 * XN)
-    ]
-
-
-def contribution_kernel(region_ref, pattern_ref, window_ref, integrals_ref, out_ref, sa_ref, sb_ref):
+def chip_offset(chip, x):
+    distance, phase = ((1, 0), (1, 1), (2, 0), (2, 1))[x]
+    return distance if (chip // distance + phase) % 2 == 0 else -distance
+
+
+def chip_pairs(regions, zlo):
+    chips = regions // 2
+    pairs = []
+    for region in range(regions):
+        for group in range(2 * XN):
+            chip, core = region // 2, region % 2
+            offset = chip_offset(chip, group % XN)
+            z = ((group // XN) * zlo + chip % zlo + offset) % (2 * zlo)
+            target = ((chip + offset) % chips) * 2 + core
+            pairs.append((region * 2 * XN + group, target * 2 * XN + (z // zlo) * XN + group % XN))
+    return pairs
+
+
+def contribution_kernel(region_ref, pattern_ref, window_ref, own_ref, integrals_ref, out_ref, sa_ref, sb_ref):
     region = region_ref[0]
     a = [pattern_ref[0, 0, t, 2] for t in range(NT)]
     live = [pattern_ref[0, 0, t, 3] for t in range(NT)]
@@ -50,15 +44,18 @@
     low8 = lane8 < 64
 
     def tile(t, want_high):
-        offset = (pattern_ref[0, 0, t, 0] - region + 64 + REACH) % 64 - REACH
+        source = pattern_ref[0, 0, t, 0]
+        offset = (source // 2 - region // 2 + 32 + 2) % 32 - 2
         distance = jnp.abs(offset)
-        place = jnp.where(distance == 2, region // 2, region)
-        phase = jnp.where(offset > 0, place % 2, 1 - place % 2)
+        phase = jnp.where(distance == 2, region // 4, region // 2) % 2
+        phase = jnp.where(offset > 0, phase, 1 - phase)
         x = jnp.where(distance == 2, 2, 0) + phase
-        x = jnp.where(distance == 0, 2, x)
-        j = jnp.where(distance == 1, 0, jnp.where(distance == 2, 0, 1))
+        other = (source % 2) ^ (region % 2)
         m = pattern_ref[0, 0, t, 1]
-        part = window_ref[x, j, :, pl.ds(pl.multiple_of((m // 2) * 128, 128), 128)].astype(F32)
+        lanes = pl.ds(pl.multiple_of((m // 2) * 128, 128), 128)
+        away = window_ref[x, other, :, lanes].astype(F32)
+        home = own_ref[other, :, lanes].astype(F32)
+        part = jnp.where(offset == 0, home, away)
         return pltpu.roll(part, 64 * ((m % 2) ^ want_high), 1)
 
     chunk0 = jnp.where(low8, tile(0, 0), tile(1, 1))
@@ -198,27 +195,35 @@
         value = jnp.broadcast_to(value[None], (XN,) + value.shape)
         return lax.all_to_all(value, "grp", 0, 0, axis_index_groups=groups)
 
-    pairs = [request_pairs(j, regions) for j in range(2)]
-    asked = [lax.ppermute(support, axes, pairs[j]) for j in range(2)]
-    asked = jnp.concatenate(asked, axis=1)[0]
-    pick = (asked[:, None] == jnp.arange(occupied.shape[1], dtype=jnp.int32)[None, :]).astype(BF16)
-    selected = lax.dot_general(pick, occupied, NT_DIMS, preferred_element_type=F32).astype(BF16)
-    back = [[(d, s) for s, d in p] for p in pairs]
-    got = [lax.ppermute(selected[j * OSUP : (j + 1) * OSUP], axes, back[j]) for j in range(2)]
-    window = spread(jnp.stack(got, 0))
+    def pick(orbitals):
+        wanted = orbitals[0][:, None] == jnp.arange(occupied.shape[1], dtype=jnp.int32)[None, :]
+        out = lax.dot_general(wanted.astype(BF16), occupied, NT_DIMS, preferred_element_type=F32)
+        return out.astype(BF16)
+
+    sibling = [(r, r ^ 1) for r in range(regions)]
+    partner = chip_pairs(regions, 8)
+    both = jnp.concatenate([support, lax.ppermute(support, "blk", sibling)], axis=1)
+    asked = lax.ppermute(both, axes, partner)
+    mine = pick(both)
+    answer = lax.ppermute(pick(asked), axes, partner)
+    fromsib = lax.ppermute(
+        jnp.concatenate([answer[OSUP:], mine[OSUP:]], axis=0), "blk", sibling
+    )
+    window = spread(jnp.stack([answer[:OSUP], fromsib[:OSUP]], 0))
+    own = jnp.stack([mine[:OSUP], fromsib[OSUP:]], 0)
 
     message = pl.pallas_call(
         contribution_kernel,
         out_shape=jax.ShapeDtypeStruct((ROWS, 128), BF16),
-        in_specs=[smem(), smem(), vmem(), vmem()],
+        in_specs=[smem(), smem(), vmem(), vmem(), vmem()],
         out_specs=vmem(),
         scratch_shapes=[pltpu.VMEM((512, 128), F32), pltpu.VMEM((256, 128), F32)],
         name="contribution",
-    )(region, pattern, in_vmem(window), integrals)
+    )(region, pattern, in_vmem(window), in_vmem(own), in_vmem(integrals))
 
     far = lax.ppermute(message, "grp", [(g, (g + XN) % (2 * XN)) for g in range(2 * XN)])
     everyone = spread(message)
-    metric = metric_inv.reshape(AUXR // AB, AB, AUXR)
+    metric = in_vmem(metric_inv.reshape(AUXR // AB, AB, AUXR))
     early = pl.pallas_call(
         early_kernel,
         out_shape=jax.ShapeDtypeStruct((BF, XN * BF), F32),

time: 90.1 us -> 94.8 us (1.052)
  Pallas kernels: 11.7 us -> 8.62 us
  matrix products: 0.37 us -> 3.19 us
  starting transfers between devices: 45.8 us -> 48.3 us
  waiting for transfers between devices: 27.6 us -> 29.1 us
  other arithmetic: 0.08 us -> 1.48 us
    all_to_all x2, starting transfers between devices: 6.78 us -> 17.3 us  [spread(): return lax.all_to_all(value, 'grp', 0, 0, axis_index_groups=groups)]
    ppermute x4, starting transfers between devices: 25.9 us -> 18.7 us  [the longest x1 8.87 us: per_device(): lax.ppermute(support, 'blk', sibling)]
    dot_general x1 -> x2, matrix products: 0.37 us -> 3.19 us  [pick(): lax.dot_general(wanted.astype(BF16), occupied, NT_DIMS, preferred_element...]
    pallas_call x1, Pallas kernels: 3.53 us -> 1.94 us  [per_device(): pl.pallas_call(late_kernel, out_shape=jax.ShapeDtypeStruct((XN, BF // 2,...]
    all_to_all x2, waiting for transfers between devices: 3.19 us -> 4.48 us  [spread(): return lax.all_to_all(value, 'grp', 0, 0, axis_index_groups=groups)]
  transfers between devices with their start and end apart: 8 -> 8, of which waited for: 5 -> 7; matrix products, arithmetic and copies ran while one was open for 1% -> 3% of each run, Pallas kernels for 4% -> 3%
where the time goes in v1:
time: 94.8 us; the launch traced here: 94.2 us
  starting transfers between devices  48.3 us (51%)
  waiting for transfers between devices  29.1 us (31%)
  Pallas kernels  8.62 us (9%)
  local copies, waits for them, and re-layouts  3.33 us (4%)
  matrix products  3.19 us (3%)
  other arithmetic  1.48 us (2%)
    ppermute x1, waiting for transfers between devices, per_device(): lax.ppermute(message, 'grp', [(g, (g + XN) % (2 * XN)) for g in range(2 *...  20.9 us
    all_to_all x2, starting transfers between devices, spread(): return lax.all_to_all(value, 'grp', 0, 0, axis_index_groups=groups)  17.3 us
    ppermute x1, starting transfers between devices, per_device(): lax.ppermute(support, 'blk', sibling)  8.87 us
    ppermute x1, starting transfers between devices, per_device(): lax.ppermute(message, 'grp', [(g, (g + XN) % (2 * XN)) for g in range(2 *...  8.47 us
    ppermute x1, starting transfers between devices, per_device(): lax.ppermute(jnp.concatenate([answer[OSUP:], mine[OSUP:]], axis=0), 'blk'...  4.54 us
    all_to_all x2, waiting for transfers between devices, spread(): return lax.all_to_all(value, 'grp', 0, 0, axis_index_groups=groups)  4.48 us
    all_to_all x1, starting transfers between devices, per_device(): late = lax.all_to_all(late, 'grp', 0, 0, axis_index_groups=groups)  3.9 us
    ppermute x1, starting transfers between devices, per_device(): answer = lax.ppermute(pick(asked), axes, partner)  3.34 us
  transfers between devices with their start and end apart: 8, of which 7 were waited for; matrix products, arithmetic and copies ran while one was open for 3% of the time, Pallas kernels for 3%

profile of v1, /device:TPU:1, one launch (start us, length us, event | category | flops | bytes accessed | tf_op | source)
XLA Modules:
  0.0 94.2 jit_solution(17776375887735598413)
XLA Ops:
  0.0 8.9 %collective-permute-start = (s32[1,8]{1,0:T(1,128)}, s32[1,8]{1,0:T(1,128)S(1)}, u32[]{:S(2)}, u32[]{:S(2)}) collective-permute-start(s32[1,8]{1,0:T(1,128)} %param.9), channel_id=1, source_target_pairs={{0,8},{8,0},{16,24},{24,16},{32,40},{40,32},{48,56},{56,48},{64,72... | collective-permute-start | bytes 104 | tf_op jit(solution)/shard_map/ppermute | solution.py:205
  8.9 0.9 collective-permute-done
  9.8 0.7 pad_add_fusion
  10.5 1.9 %collective-permute-start.1 = (s32[1,16]{1,0:T(1,128)S(1)}, s32[1,16]{1,0:T(1,128)S(1)}, u32[]{:S(2)}, u32[]{:S(2)}) collective-permute-start(s32[1,16]{1,0:T(1,128)S(1)} %pad_add_fusion), channel_id=1, source_target_pairs={{0,16},{1,501},{2,34},{3,487},{4,20},{5,497},{6,38},{7,483},{8,24}... | collective-permute-start | bytes 200 | tf_op jit(solution)/shard_map/ppermute | solution.py:206
  12.5 0.7 fusion.4
  13.2 1.6 %convolution_convert_fusion = bf16[16,512]{1,0:T(8,128)(2,1)S(1)} fusion(bf16[512,1024]{1,0:T(8,128)(2,1)} %param.5, s32[16]{0:T(128)S(1)} %fusion.4), kind=kOutput, calls=%fused_computation | convolution fusion | flops 16801792 | bytes 1065024 | tf_op jit(solution)/shard_map/dot_general | solution.py:200
  14.8 1.6 %convolution_convert_fusion.1 = bf16[16,512]{1,0:T(8,128)(2,1)S(1)} fusion(bf16[512,1024]{1,0:T(8,128)(2,1)} %param.5, s32[16]{0:T(128)S(1)} %bitcast.18), kind=kOutput, calls=%fused_computation.1 | convolution fusion | flops 16801792 | bytes 1065024 | tf_op jit(solution)/shard_map/dot_general | solution.py:200
  16.4 3.3 %collective-permute-start.2 = (bf16[16,512]{1,0:T(8,128)(2,1)S(1)}, bf16[16,512]{1,0:T(8,128)(2,1)S(1)}, u32[]{:S(2)}, u32[]{:S(2)}) collective-permute-start(bf16[16,512]{1,0:T(8,128)(2,1)S(1)} %convolution_convert_fusion.1), channel_id=1, source_target_pairs={{0,16},{1,501},{2,34},{3,487},{4,20},{5,497},{6,38},{7,483},{8,24}... | collective-permute-start | bytes 49160 | tf_op jit(solution)/shard_map/ppermute | solution.py:208
  19.8 1.1 %collective-permute-done.2 = bf16[16,512]{1,0:T(8,128)(2,1)S(1)} collective-permute-done((bf16[16,512]{1,0:T(8,128)(2,1)S(1)}, bf16[16,512]{1,0:T(8,128)(2,1)S(1)}, u32[]{:S(2)}, u32[]{:S(2)}) %collective-permute-start.2) | collective-permute-done | bytes 16416 | tf_op jit(solution)/shard_map/ppermute | solution.py:208
  20.9 4.5 %collective-permute-start.3 = (bf16[16,512]{1,0:T(8,128)(2,1)S(1)}, bf16[16,512]{1,0:T(8,128)(2,1)S(1)}, u32[]{:S(2)}, u32[]{:S(2)}) collective-permute-start(bf16[16,512]{1,0:T(8,128)(2,1)S(1)} %pad_maximum_fusion), channel_id=1, source_target_pairs={{0,8},{8,0},{16,24},{24,16},{32,40},{40,32},{48,56},{56,48},{64,72... | collective-permute-start | bytes 49160 | tf_op jit(solution)/shard_map/ppermute | solution.py:209
  25.5 0.6 copy.6.pattern_ref
  26.3 0.6 broadcast_in_dim.4
  27.0 13.8 %all-to-all-start = ((bf16[4,2,8,512]{3,2,1,0:T(8,128)(2,1)}), bf16[4,2,8,512]{3,2,1,0:T(8,128)(2,1)S(1)}, u32[]{:S(2)}, u32[]{:S(2)}) async-start(bf16[4,2,8,512]{3,2,1,0:T(8,128)(2,1)} %broadcast_in_dim.4), calls=%async_computation | async-start | bytes 131072 | tf_op jit(solution)/shard_map/all_to_all | solution.py:196
  40.8 4.5 %all-to-all-done.window_ref = bf16[4,2,8,512]{3,2,1,0:T(8,128)(2,1)S(1)} async-done(((bf16[4,2,8,512]{3,2,1,0:T(8,128)(2,1)}), bf16[4,2,8,512]{3,2,1,0:T(8,128)(2,1)S(1)}, u32[]{:S(2)}, u32[]{:S(2)}) %all-to-all-start) | async-done | bytes 65568 | tf_op jit(solution)/shard_map/all_to_all | solution.py:196
  45.2 2.1 %contribution.1.own_ref = bf16[784,128]{1,0:T(8,128)(2,1)} custom-call(s32[1]{0:T(128)} %bitcast.1.region_ref, s32[1,1,3,4]{3,2,1,0:T(4,128)} %copy.6.pattern_ref, bf16[4,2,8,512]{3,2,1,0:T(8,128)(2,1)S(1)} %all-to-all-done.window_ref, bf16[2,8,512]{2,1,0:T(8,128)(2,1)S(1)} %pad_maximum_fusion.2.own_ref, bf16[1,1,3,64,4096]{4,3,2,1,0:T(8,128)(2,1)S(1)} %copy-done.1), custom_call_target="tpu_custom_call" | custom-call | tf_op jit(solution)/shard_map/contribution/pallas_call | solution.py:215
  47.3 2.1 %broadcast_in_dim.5 = bf16[4,784,128]{2,1,0:T(8,128)(2,1)} broadcast(bf16[784,128]{1,0:T(8,128)(2,1)} %contribution.1.own_ref), dimensions={1,2} | broadcast | bytes 1003520 | tf_op jit(solution)/shard_map/broadcast_in_dim | solution.py:195
  49.4 3.5 %all-to-all-start.1 = ((bf16[4,784,128]{2,1,0:T(8,128)(2,1)}), bf16[4,784,128]{2,1,0:T(8,128)(2,1)S(1)}, u32[]{:S(2)}, u32[]{:S(2)}) async-start(bf16[4,784,128]{2,1,0:T(8,128)(2,1)} %broadcast_in_dim.5), calls=%async_computation.1 | async-start | bytes 1605632 | tf_op jit(solution)/shard_map/all_to_all | solution.py:196
  52.9 8.5 %collective-permute-start.4 = (bf16[784,128]{1,0:T(8,128)(2,1)S(1)}, bf16[784,128]{1,0:T(8,128)(2,1)S(1)}, u32[]{:S(2)}, u32[]{:S(2)}) collective-permute-start(bf16[784,128]{1,0:T(8,128)(2,1)S(1)} %copy-done.2), channel_id=1, source_target_pairs={{0,4},{1,5},{2,6},{3,7},{4,0},{5,1},{6,2},{7,3},{8,12},{9,13},{10,... | collective-permute-start | bytes 602120 | tf_op jit(solution)/shard_map/ppermute | solution.py:224
  61.4 20.9 %collective-permute-done.4.far_ref = bf16[784,128]{1,0:T(8,128)(2,1)S(1)} collective-permute-done((bf16[784,128]{1,0:T(8,128)(2,1)S(1)}, bf16[784,128]{1,0:T(8,128)(2,1)S(1)}, u32[]{:S(2)}, u32[]{:S(2)}) %collective-permute-start.4) | collective-permute-done | bytes 200736 | tf_op jit(solution)/shard_map/ppermute | solution.py:224
  82.3 1.9 %late.1 = f32[4,32,128]{2,1,0:T(8,128)} custom-call(bf16[784,128]{1,0:T(8,128)(2,1)S(1)} %collective-permute-done.4.far_ref, bf16[4,784,128]{2,1,0:T(8,128)(2,1)S(1)} %all-to-all-done.1.all_ref, bf16[16,64,1024]{2,1,0:T(8,128)(2,1)S(1)} %bitcast.16), custom_call_target="tpu_custom_call" | custom-call | tf_op jit(solution)/shard_map/late/pallas_call | solution.py:234
  84.2 3.9 %all-to-all-start.2 = ((f32[4,32,128]{2,1,0:T(8,128)}), f32[4,32,128]{2,1,0:T(8,128)S(1)}, u32[]{:S(2)}, u32[]{:S(2)}) async-start(f32[4,32,128]{2,1,0:T(8,128)} %late.1), calls=%async_computation.2 | async-start | bytes 131072 | tf_op jit(solution)/shard_map/all_to_all | solution.py:241
  88.1 3.0 %early.1.early_ref = f32[64,256]{1,0:T(8,128)} custom-call(bf16[784,128]{1,0:T(8,128)(2,1)} %contribution.1.own_ref, bf16[4,784,128]{2,1,0:T(8,128)(2,1)S(1)} %all-to-all-done.1.all_ref, bf16[16,64,1024]{2,1,0:T(8,128)(2,1)S(1)} %bitcast.17), custom_call_target="tpu_custom_call" | custom-call | tf_op jit(solution)/shard_map/early/pallas_call | solution.py:227
  91.1 1.4 %all-to-all-done.2.late_ref = f32[4,32,128]{2,1,0:T(8,128)S(1)} async-done(((f32[4,32,128]{2,1,0:T(8,128)}), f32[4,32,128]{2,1,0:T(8,128)S(1)}, u32[]{:S(2)}, u32[]{:S(2)}) %all-to-all-start.2) | async-done | bytes 65568 | tf_op jit(solution)/shard_map/all_to_all | solution.py:241
  92.6 1.6 %join.1 = f32[64,512]{1,0:T(8,128)} custom-call(s32[1]{0:T(128)} %bitcast.group_ref, f32[64,256]{1,0:T(8,128)} %early.1.early_ref, f32[4,32,128]{2,1,0:T(8,128)S(1)} %all-to-all-done.2.late_ref), custom_call_target="tpu_custom_call" | custom-call | tf_op jit(solution)/shard_map/join/pallas_call | solution.py:242
  (17 shorter events, 0.3 us)
Async XLA Ops:
  0.0 25.5 %copy-start.3 = (s32[1,1,3,4]{3,1,2,0:T(1,128)S(1)}, s32[1,1,3,4]{3,1,2,0:T(1,128)}, u32[]{:S(2)}) copy-start(s32[1,1,3,4]{3,1,2,0:T(1,128)} %param.8) | copy-start | bytes 148
  0.0 45.2 %copy-start.1 = (bf16[1,1,3,64,4096]{4,3,2,1,0:T(8,128)(2,1)S(1)}, bf16[1,1,3,64,4096]{4,3,2,1,0:T(8,128)(2,1)}, u32[]{:S(2)}) copy-start(bf16[1,1,3,64,4096]{4,3,2,1,0:T(8,128)(2,1)} %integrals_ref.1) | copy-start | bytes 4718596
  0.0 9.8 %collective-permute-start = (s32[1,8]{1,0:T(1,128)}, s32[1,8]{1,0:T(1,128)S(1)}, u32[]{:S(2)}, u32[]{:S(2)}) collective-permute-start(s32[1,8]{1,0:T(1,128)} %param.9), channel_id=1, source_target_pairs={{0,8},{8,0},{16,24},{24,16},{32,40},{40,32},{48,56},{56,48},{64,72... | collective-permute-start | bytes 104 | tf_op jit(solution)/shard_map/ppermute | solution.py:205
  10.5 4.3 %collective-permute-start.1 = (s32[1,16]{1,0:T(1,128)S(1)}, s32[1,16]{1,0:T(1,128)S(1)}, u32[]{:S(2)}, u32[]{:S(2)}) collective-permute-start(s32[1,16]{1,0:T(1,128)S(1)} %pad_add_fusion), channel_id=1, source_target_pairs={{0,16},{1,501},{2,34},{3,487},{4,20},{5,497},{6,38},{7,483},{8,24}... | collective-permute-start | bytes 200 | tf_op jit(solution)/shard_map/ppermute | solution.py:206
  16.4 4.5 %collective-permute-start.2 = (bf16[16,512]{1,0:T(8,128)(2,1)S(1)}, bf16[16,512]{1,0:T(8,128)(2,1)S(1)}, u32[]{:S(2)}, u32[]{:S(2)}) collective-permute-start(bf16[16,512]{1,0:T(8,128)(2,1)S(1)} %convolution_convert_fusion.1), channel_id=1, source_target_pairs={{0,16},{1,501},{2,34},{3,487},{4,20},{5,497},{6,38},{7,483},{8,24}... | collective-permute-start | bytes 49160 | tf_op jit(solution)/shard_map/ppermute | solution.py:208
  20.9 5.4 %collective-permute-start.3 = (bf16[16,512]{1,0:T(8,128)(2,1)S(1)}, bf16[16,512]{1,0:T(8,128)(2,1)S(1)}, u32[]{:S(2)}, u32[]{:S(2)}) collective-permute-start(bf16[16,512]{1,0:T(8,128)(2,1)S(1)} %pad_maximum_fusion), channel_id=1, source_target_pairs={{0,8},{8,0},{16,24},{24,16},{32,40},{40,32},{48,56},{56,48},{64,72... | collective-permute-start | bytes 49160 | tf_op jit(solution)/shard_map/ppermute | solution.py:209
  27.0 18.3 %all-to-all-start = ((bf16[4,2,8,512]{3,2,1,0:T(8,128)(2,1)}), bf16[4,2,8,512]{3,2,1,0:T(8,128)(2,1)S(1)}, u32[]{:S(2)}, u32[]{:S(2)}) async-start(bf16[4,2,8,512]{3,2,1,0:T(8,128)(2,1)} %broadcast_in_dim.4), calls=%async_computation | async-start | bytes 131072 | tf_op jit(solution)/shard_map/all_to_all | solution.py:196
  47.3 5.6 %copy-start.2 = (bf16[784,128]{1,0:T(8,128)(2,1)S(1)}, bf16[784,128]{1,0:T(8,128)(2,1)}, u32[]{:S(2)}) copy-start(bf16[784,128]{1,0:T(8,128)(2,1)} %contribution.1.own_ref) | copy-start | bytes 602116
  47.3 34.9 %copy-start = (bf16[1024,1024]{1,0:T(8,128)(2,1)S(1)}, bf16[1024,1024]{1,0:T(8,128)(2,1)}, u32[]{:S(2)}) copy-start(bf16[1024,1024]{1,0:T(8,128)(2,1)} %param.7) | copy-start | bytes 6291460
  49.4 32.9 %all-to-all-start.1 = ((bf16[4,784,128]{2,1,0:T(8,128)(2,1)}), bf16[4,784,128]{2,1,0:T(8,128)(2,1)S(1)}, u32[]{:S(2)}, u32[]{:S(2)}) async-start(bf16[4,784,128]{2,1,0:T(8,128)(2,1)} %broadcast_in_dim.5), calls=%async_computation.1 | async-start | bytes 1605632 | tf_op jit(solution)/shard_map/all_to_all | solution.py:196
  52.9 29.3 %collective-permute-start.4 = (bf16[784,128]{1,0:T(8,128)(2,1)S(1)}, bf16[784,128]{1,0:T(8,128)(2,1)S(1)}, u32[]{:S(2)}, u32[]{:S(2)}) collective-permute-start(bf16[784,128]{1,0:T(8,128)(2,1)S(1)} %copy-done.2), channel_id=1, source_target_pairs={{0,4},{1,5},{2,6},{3,7},{4,0},{5,1},{6,2},{7,3},{8,12},{9,13},{10,... | collective-permute-start | bytes 602120 | tf_op jit(solution)/shard_map/ppermute | solution.py:224
  84.2 8.4 %all-to-all-start.2 = ((f32[4,32,128]{2,1,0:T(8,128)}), f32[4,32,128]{2,1,0:T(8,128)S(1)}, u32[]{:S(2)}, u32[]{:S(2)}) async-start(f32[4,32,128]{2,1,0:T(8,128)} %late.1), calls=%async_computation.2 | async-start | bytes 131072 | tf_op jit(solution)/shard_map/all_to_all | solution.py:241

commit v2 on v1

--- a/solution.py
+++ b/solution.py
@@ -11,6 +11,7 @@
 AUXR = 1024
 OSUP = 8
 NT = 3
+REACH = 3
 XN = 4
 DATA = OSUP * BF * NT * AB // 128
 ROWS = DATA + 16
@@ -18,25 +19,23 @@
 BF16 = jnp.bfloat16
 
 
-def chip_offset(chip, x):
-    distance, phase = ((1, 0), (1, 1), (2, 0), (2, 1))[x]
-    return distance if (chip // distance + phase) % 2 == 0 else -distance
-
-
-def chip_pairs(regions, zlo):
-    chips = regions // 2
+TASKS = (((3, 0), (3, 1), (2, 0), (2, 1)), ((1, 0), (0, 0), (1, 1), (0, 0)))
+
+
+def swap_pairs(j, regions, zlo):
     pairs = []
     for region in range(regions):
         for group in range(2 * XN):
-            chip, core = region // 2, region % 2
-            offset = chip_offset(chip, group % XN)
-            z = ((group // XN) * zlo + chip % zlo + offset) % (2 * zlo)
-            target = ((chip + offset) % chips) * 2 + core
-            pairs.append((region * 2 * XN + group, target * 2 * XN + (z // zlo) * XN + group % XN))
+            distance, phase = TASKS[j][group % XN]
+            place = (region // 2 if distance == 2 else region) + phase
+            target = region + (distance if place % 2 == 0 else -distance)
+            z = (group // XN) * zlo + (region // 2) % zlo + target // 2 - region // 2
+            copy = (z % (2 * zlo)) // zlo * XN + group % XN
+            pairs.append((region * 2 * XN + group, (target % regions) * 2 * XN + copy))
     return pairs
 
 
-def contribution_kernel(region_ref, pattern_ref, window_ref, own_ref, integrals_ref, out_ref, sa_ref, sb_ref):
+def contribution_kernel(region_ref, pattern_ref, window_ref, integrals_ref, out_ref, all_ref, sa_ref, sb_ref):
     region = region_ref[0]
     a = [pattern_ref[0, 0, t, 2] for t in range(NT)]
     live = [pattern_ref[0, 0, t, 3] for t in range(NT)]
@@ -45,17 +44,16 @@
 
     def tile(t, want_high):
         source = pattern_ref[0, 0, t, 0]
-        offset = (source // 2 - region // 2 + 32 + 2) % 32 - 2
+        offset = (source - region + 64 + REACH) % 64 - REACH
         distance = jnp.abs(offset)
-        phase = jnp.where(distance == 2, region // 4, region // 2) % 2
-        phase = jnp.where(offset > 0, phase, 1 - phase)
-        x = jnp.where(distance == 2, 2, 0) + phase
-        other = (source % 2) ^ (region % 2)
+        place = jnp.where(distance == 2, region // 2, region) % 2
+        phase = jnp.where(offset > 0, place, 1 - place)
+        x = jnp.where(distance == 3, phase, jnp.where(distance == 0, 1, 2 * phase))
+        x = jnp.where(distance == 2, 2 + phase, x)
+        j = jnp.where(distance > 1, 0, 1)
         m = pattern_ref[0, 0, t, 1]
         lanes = pl.ds(pl.multiple_of((m // 2) * 128, 128), 128)
-        away = window_ref[x, other, :, lanes].astype(F32)
-        home = own_ref[other, :, lanes].astype(F32)
-        part = jnp.where(offset == 0, home, away)
+        part = window_ref[x, j, :, lanes].astype(F32)
         return pltpu.roll(part, 64 * ((m % 2) ^ want_high), 1)
 
     chunk0 = jnp.where(low8, tile(0, 0), tile(1, 1))
@@ -80,11 +78,28 @@
         sa_ref[pl.ds(2 * k + 1, OSUP, stride=BF), :] = jnp.where(low8, s0, v[1])
         sb_ref[pl.ds(2 * k, OSUP // 2, stride=BF), :] = jnp.where(low8, v[2], half_s)[: OSUP // 2]
         sb_ref[pl.ds(2 * k + 1, OSUP // 2, stride=BF), :] = jnp.where(low8, s2, half)[: OSUP // 2]
-    out_ref[0:512, :] = sa_ref[...].astype(BF16)
-    out_ref[512:768, :] = sb_ref[...].astype(BF16)
+    a_part = sa_ref[...].astype(BF16)
+    b_part = sb_ref[...].astype(BF16)
     lane = lax.broadcasted_iota(jnp.int32, (16, 128), 1)
-    tag = jnp.where(lane == 0, a[0], jnp.where(lane == 1, a[1], a[2]))
-    out_ref[768:784, :] = tag.astype(F32).astype(BF16)
+    tag = jnp.where(lane == 0, a[0], jnp.where(lane == 1, a[1], a[2])).astype(F32).astype(BF16)
+    out_ref[0:512, :] = a_part
+    out_ref[512:768, :] = b_part
+    out_ref[768:784, :] = tag
+    for copy in range(XN):
+        all_ref[copy, 0:512, :] = a_part
+        all_ref[copy, 512:768, :] = b_part
+        all_ref[copy, 768:784, :] = tag
+
+
+def stage_kernel(*refs):
+    half = len(refs) // 3
+    copies = [
+        pltpu.make_async_copy(refs[k], refs[half + k], refs[2 * half + k]) for k in range(half)
+    ]
+    for copy in copies:
+        copy.start()
+    for copy in copies:
+        copy.wait()
 
 
 def blocks_of(tag_row):
@@ -184,6 +199,17 @@
     return pltpu.with_memory_space_constraint(value, pltpu.VMEM)
 
 
+def staged(parts):
+    return pl.pallas_call(
+        stage_kernel,
+        out_shape=[pltpu.VMEM(p.shape, p.dtype) for p in parts],
+        in_specs=[pl.BlockSpec(memory_space=pltpu.HBM)] * len(parts),
+        out_specs=[vmem()] * len(parts),
+        scratch_shapes=[pltpu.SemaphoreType.DMA] * len(parts),
+        compiler_params=pltpu.CompilerParams(vmem_limit_bytes=16 * 2**20),
+    )(*[pltpu.with_memory_space_constraint(p, pltpu.HBM) for p in parts])
+
+
 def per_device(occupied, integrals, metric_inv, pattern, support):
     regions = lax.axis_size("blk")
     axes = ("blk", "grp")
@@ -195,48 +221,50 @@
         value = jnp.broadcast_to(value[None], (XN,) + value.shape)
         return lax.all_to_all(value, "grp", 0, 0, axis_index_groups=groups)
 
-    def pick(orbitals):
-        wanted = orbitals[0][:, None] == jnp.arange(occupied.shape[1], dtype=jnp.int32)[None, :]
-        out = lax.dot_general(wanted.astype(BF16), occupied, NT_DIMS, preferred_element_type=F32)
-        return out.astype(BF16)
-
-    sibling = [(r, r ^ 1) for r in range(regions)]
-    partner = chip_pairs(regions, 8)
-    both = jnp.concatenate([support, lax.ppermute(support, "blk", sibling)], axis=1)
-    asked = lax.ppermute(both, axes, partner)
-    mine = pick(both)
-    answer = lax.ppermute(pick(asked), axes, partner)
-    fromsib = lax.ppermute(
-        jnp.concatenate([answer[OSUP:], mine[OSUP:]], axis=0), "blk", sibling
-    )
-    window = spread(jnp.stack([answer[:OSUP], fromsib[:OSUP]], 0))
-    own = jnp.stack([mine[:OSUP], fromsib[OSUP:]], 0)
-
-    message = pl.pallas_call(
+    pairs = [swap_pairs(j, regions, 8) for j in range(2)]
+    asked = []
+    for j in range(2):
+        asked.append(lax.ppermute(support, axes, pairs[j]))
+    occupied, integrals = staged([occupied, integrals])
+    asked = jnp.concatenate(asked, axis=1)[0]
+    wanted = asked[:, None] == jnp.arange(occupied.shape[1], dtype=jnp.int32)[None, :]
+    answer = lax.dot_general(wanted.astype(BF16), occupied, NT_DIMS, preferred_element_type=F32)
+    answer = answer.astype(BF16)
+    answer = [lax.ppermute(answer[j * OSUP : (j + 1) * OSUP], axes, pairs[j]) for j in range(2)]
+    window = spread(jnp.stack(answer, 0))
+    (metric,) = staged([metric_inv])
+    metric = in_vmem(metric.reshape(AUXR // AB, AB, AUXR))
+
+    message, copies = pl.pallas_call(
         contribution_kernel,
-        out_shape=jax.ShapeDtypeStruct((ROWS, 128), BF16),
-        in_specs=[smem(), smem(), vmem(), vmem(), vmem()],
-        out_specs=vmem(),
+        out_shape=[
+            pltpu.VMEM((ROWS, 128), BF16),
+            jax.ShapeDtypeStruct((XN, ROWS, 128), BF16),
+        ],
+        in_specs=[smem(), smem(), vmem(), vmem()],
+        out_specs=[vmem(), vmem()],
         scratch_shapes=[pltpu.VMEM((512, 128), F32), pltpu.VMEM((256, 128), F32)],
         name="contribution",
-    )(region, pattern, in_vmem(window), in_vmem(own), in_vmem(integrals))
+            compiler_params=pltpu.CompilerParams(vmem_limit_bytes=16 * 2**20),
+    )(region, pattern, in_vmem(window), in_vmem(integrals))
 
     far = lax.ppermute(message, "grp", [(g, (g + XN) % (2 * XN)) for g in range(2 * XN)])
-    everyone = spread(message)
-    metric = in_vmem(metric_inv.reshape(AUXR // AB, AB, AUXR))
+    everyone = lax.all_to_all(copies, "grp", 0, 0, axis_index_groups=groups)
     early = pl.pallas_call(
         early_kernel,
         out_shape=jax.ShapeDtypeStruct((BF, XN * BF), F32),
         in_specs=[vmem(), vmem(), vmem()],
         out_specs=vmem(),
         name="early",
-    )(message, in_vmem(everyone), metric)
+        compiler_params=pltpu.CompilerParams(vmem_limit_bytes=16 * 2**20),
+    )(in_vmem(message), in_vmem(everyone), metric)
     late = pl.pallas_call(
         late_kernel,
         out_shape=jax.ShapeDtypeStruct((XN, BF // 2, 2 * BF), F32),
         in_specs=[vmem(), vmem(), vmem()],
         out_specs=vmem(),
         name="late",
+            compiler_params=pltpu.CompilerParams(vmem_limit_bytes=16 * 2**20),
     )(in_vmem(far), in_vmem(everyone), metric)
     late = lax.all_to_all(late, "grp", 0, 0, axis_index_groups=groups)
     return pl.pallas_call(
@@ -245,6 +273,7 @@
         in_specs=[smem(), vmem(), vmem()],
         out_specs=vmem(),
         name="join",
+            compiler_params=pltpu.CompilerParams(vmem_limit_bytes=16 * 2**20),
     )(group, early, in_vmem(late))
 
 

time: 94.8 us -> 83.4 us (0.88)
  the two profiles are of different devices: /device:TPU:1 before, /device:TPU:2 now
where the time goes in v2:
time: 83.4 us; the launch traced here: 82.9 us
  starting transfers between devices  47.7 us (57%)
  waiting for transfers between devices  24.3 us (29%)
  Pallas kernels  9.7 us (12%)
    ppermute x2, starting transfers between devices, per_device(): asked.append(lax.ppermute(support, axes, pairs[j]))  15.2 us
    ppermute x1, waiting for transfers between devices, per_device(): lax.ppermute(message, 'grp', [(g, (g + XN) % (2 * XN)) for g in range(2 *...  15.1 us
    ppermute x1, starting transfers between devices, per_device(): lax.ppermute(message, 'grp', [(g, (g + XN) % (2 * XN)) for g in range(2 *...  9.27 us
    ppermute x2, starting transfers between devices, per_device(): lax.ppermute(answer[j * OSUP:(j + 1) * OSUP], axes, pairs[j])  6.82 us
    all_to_all x1, starting transfers between devices, spread(): return lax.all_to_all(value, 'grp', 0, 0, axis_index_groups=groups)  6.74 us
    all_to_all x1, starting transfers between devices, per_device(): everyone = lax.all_to_all(copies, 'grp', 0, 0, axis_index_groups=groups)  4.92 us
    all_to_all x1, starting transfers between devices, per_device(): late = lax.all_to_all(late, 'grp', 0, 0, axis_index_groups=groups)  4.8 us
    all_to_all x1, waiting for transfers between devices, spread(): return lax.all_to_all(value, 'grp', 0, 0, axis_index_groups=groups)  4.16 us
  transfers between devices with their start and end apart: 8, of which 4 were waited for; matrix products, arithmetic and copies ran while one was open for 0% of the time, Pallas kernels for 6%

profile of v2, /device:TPU:2, one launch (start us, length us, event | category | flops | bytes accessed | tf_op | source)
XLA Modules:
  0.0 82.9 jit_solution(13549156246074400108)
XLA Ops:
  0.0 13.9 %collective-permute-start = (s32[1,8]{1,0:T(1,128)}, s32[1,8]{1,0:T(1,128)S(1)}, u32[]{:S(2)}, u32[]{:S(2)}) collective-permute-start(s32[1,8]{1,0:T(1,128)} %param.9), channel_id=1, source_target_pairs={{0,24},{1,493},{2,18},{3,503},{4,28},{5,489},{6,22},{7,499},{8,500... | collective-permute-start | bytes 104 | tf_op jit(solution)/shard_map/ppermute | solution.py:227
  13.9 1.3 %collective-permute-start.1 = (s32[1,8]{1,0:T(1,128)}, s32[1,8]{1,0:T(1,128)S(1)}, u32[]{:S(2)}, u32[]{:S(2)}) collective-permute-start(s32[1,8]{1,0:T(1,128)} %param.9), channel_id=1, source_target_pairs={{0,8},{1,1},{2,510},{3,3},{4,12},{5,5},{6,506},{7,7},{8,0},{9,9},{... | collective-permute-start | bytes 104 | tf_op jit(solution)/shard_map/ppermute | solution.py:227
  15.2 1.7 %shard_map.55 = (bf16[512,1024]{1,0:T(8,128)(2,1)S(1)}, bf16[1,1,3,64,4096]{4,3,2,1,0:T(8,128)(2,1)S(1)}) custom-call(bf16[512,1024]{1,0:T(8,128)(2,1)} %refs_0_.2, bf16[1,1,3,64,4096]{4,3,2,1,0:T(8,128)(2,1)} %refs_1_.1), custom_call_target="tpu_custom_call" | custom-call | tf_op jit(solution)/shard_map/pallas_call | solution.py:203
  16.9 0.0 collective-permute-done
  16.9 0.0 collective-permute-done.1
  17.0 0.1 add_bitcast_fusion
  17.0 0.4 convolution_convert_fusion
  17.4 6.2 %collective-permute-start.2 = (bf16[8,512]{1,0:T(8,128)(2,1)S(1)}, bf16[8,512]{1,0:T(8,128)(2,1)S(1)}, u32[]{:S(2)}, u32[]{:S(2)}) collective-permute-start(bf16[8,512]{1,0:T(8,128)(2,1)S(1)} %get-tuple-element.13), channel_id=1, source_target_pairs={{0,24},{1,493},{2,18},{3,503},{4,28},{5,489},{6,22},{7,499},{8,500... | collective-permute-start | bytes 24584 | tf_op jit(solution)/shard_map/ppermute | solution.py:233
  23.6 0.7 collective-permute-start.3
  24.2 2.4 %collective-permute-done.2 = bf16[8,512]{1,0:T(8,128)(2,1)S(1)} collective-permute-done((bf16[8,512]{1,0:T(8,128)(2,1)S(1)}, bf16[8,512]{1,0:T(8,128)(2,1)S(1)}, u32[]{:S(2)}, u32[]{:S(2)}) %collective-permute-start.2) | collective-permute-done | bytes 8224 | tf_op jit(solution)/shard_map/ppermute | solution.py:233
  26.6 0.0 collective-permute-done.3
  26.6 0.6 broadcast_in_dim.2
  27.3 6.7 %all-to-all-start = ((bf16[4,2,8,512]{3,2,1,0:T(8,128)(2,1)}), bf16[4,2,8,512]{3,2,1,0:T(8,128)(2,1)S(1)}, u32[]{:S(2)}, u32[]{:S(2)}) async-start(bf16[4,2,8,512]{3,2,1,0:T(8,128)(2,1)} %broadcast_in_dim.2), calls=%async_computation | async-start | bytes 131072 | tf_op jit(solution)/shard_map/all_to_all | solution.py:222
  34.0 4.2 %all-to-all-done.window_ref = bf16[4,2,8,512]{3,2,1,0:T(8,128)(2,1)S(1)} async-done(((bf16[4,2,8,512]{3,2,1,0:T(8,128)(2,1)}), bf16[4,2,8,512]{3,2,1,0:T(8,128)(2,1)S(1)}, u32[]{:S(2)}, u32[]{:S(2)}) %all-to-all-start) | async-done | bytes 65568 | tf_op jit(solution)/shard_map/all_to_all | solution.py:222
  38.2 2.2 %contribution.1 = (bf16[784,128]{1,0:T(8,128)(2,1)S(1)}, bf16[4,784,128]{2,1,0:T(8,128)(2,1)}) custom-call(s32[1]{0:T(128)} %bitcast.1.region_ref, s32[1,1,3,4]{3,2,1,0:T(4,128)S(1)} %copy.6.pattern_ref, bf16[4,2,8,512]{3,2,1,0:T(8,128)(2,1)S(1)} %all-to-all-done.window_ref, bf16[1,1,3,64,4096]{4,3,2,1,0:T(8,128)(2,1)S(1)} %get-tuple-element.10.integrals_ref), custom_call_target="tpu_custom_call" | custom-call | tf_op jit(solution)/shard_map/contribution/pallas_call | solution.py:238
  40.4 4.9 %all-to-all-start.1 = ((bf16[4,784,128]{2,1,0:T(8,128)(2,1)}), bf16[4,784,128]{2,1,0:T(8,128)(2,1)S(1)}, u32[]{:S(2)}, u32[]{:S(2)}) async-start(bf16[4,784,128]{2,1,0:T(8,128)(2,1)} %get-tuple-element.12), calls=%async_computation.1 | async-start | bytes 1605632 | tf_op jit(solution)/shard_map/all_to_all | solution.py:252
  45.3 9.3 %collective-permute-start.4 = (bf16[784,128]{1,0:T(8,128)(2,1)S(1)}, bf16[784,128]{1,0:T(8,128)(2,1)S(1)}, u32[]{:S(2)}, u32[]{:S(2)}) collective-permute-start(bf16[784,128]{1,0:T(8,128)(2,1)S(1)} %get-tuple-element.11.own_ref), channel_id=1, source_target_pairs={{0,4},{1,5},{2,6},{3,7},{4,0},{5,1},{6,2},{7,3},{8,12},{9,13},{10,... | collective-permute-start | bytes 602120 | tf_op jit(solution)/shard_map/ppermute | solution.py:251
  54.6 1.6 %shard_map.56 = bf16[1024,1024]{1,0:T(8,128)(2,1)S(1)} custom-call(bf16[1024,1024]{1,0:T(8,128)(2,1)} %refs_0_.3), custom_call_target="tpu_custom_call" | custom-call | tf_op jit(solution)/shard_map/pallas_call | solution.py:203
  56.2 15.1 %collective-permute-done.4.far_ref = bf16[784,128]{1,0:T(8,128)(2,1)S(1)} collective-permute-done((bf16[784,128]{1,0:T(8,128)(2,1)S(1)}, bf16[784,128]{1,0:T(8,128)(2,1)S(1)}, u32[]{:S(2)}, u32[]{:S(2)}) %collective-permute-start.4) | collective-permute-done | bytes 200736 | tf_op jit(solution)/shard_map/ppermute | solution.py:251
  71.2 1.9 %late.1 = f32[4,32,128]{2,1,0:T(8,128)} custom-call(bf16[784,128]{1,0:T(8,128)(2,1)S(1)} %collective-permute-done.4.far_ref, bf16[4,784,128]{2,1,0:T(8,128)(2,1)S(1)} %all-to-all-done.1.all_ref, bf16[16,64,1024]{2,1,0:T(8,128)(2,1)S(1)} %bitcast.8), custom_call_target="tpu_custom_call" | custom-call | tf_op jit(solution)/shard_map/late/pallas_call | solution.py:261
  73.2 4.8 %all-to-all-start.2 = ((f32[4,32,128]{2,1,0:T(8,128)}), f32[4,32,128]{2,1,0:T(8,128)S(1)}, u32[]{:S(2)}, u32[]{:S(2)}) async-start(f32[4,32,128]{2,1,0:T(8,128)} %late.1), calls=%async_computation.2 | async-start | bytes 131072 | tf_op jit(solution)/shard_map/all_to_all | solution.py:269
  78.0 1.5 %early.1.early_ref = f32[64,256]{1,0:T(8,128)S(1)} custom-call(bf16[784,128]{1,0:T(8,128)(2,1)S(1)} %get-tuple-element.11.own_ref, bf16[4,784,128]{2,1,0:T(8,128)(2,1)S(1)} %all-to-all-done.1.all_ref, bf16[16,64,1024]{2,1,0:T(8,128)(2,1)S(1)} %bitcast.9), custom_call_target="tpu_custom_call" | custom-call | tf_op jit(solution)/shard_map/early/pallas_call | solution.py:253
  79.5 2.7 %all-to-all-done.2.late_ref = f32[4,32,128]{2,1,0:T(8,128)S(1)} async-done(((f32[4,32,128]{2,1,0:T(8,128)}), f32[4,32,128]{2,1,0:T(8,128)S(1)}, u32[]{:S(2)}, u32[]{:S(2)}) %all-to-all-start.2) | async-done | bytes 65568 | tf_op jit(solution)/shard_map/all_to_all | solution.py:269
  82.2 0.7 join.1
  (6 shorter events, 0.0 us)
Async XLA Ops:
  0.0 34.0 %copy-start = (s32[1,1,3,4]{3,1,2,0:T(1,128)S(1)}, s32[1,1,3,4]{3,1,2,0:T(1,128)}, u32[]{:S(2)}) copy-start(s32[1,1,3,4]{3,1,2,0:T(1,128)} %param.8) | copy-start | bytes 148
  0.0 16.9 %collective-permute-start = (s32[1,8]{1,0:T(1,128)}, s32[1,8]{1,0:T(1,128)S(1)}, u32[]{:S(2)}, u32[]{:S(2)}) collective-permute-start(s32[1,8]{1,0:T(1,128)} %param.9), channel_id=1, source_target_pairs={{0,24},{1,493},{2,18},{3,503},{4,28},{5,489},{6,22},{7,499},{8,500... | collective-permute-start | bytes 104 | tf_op jit(solution)/shard_map/ppermute | solution.py:227
  13.9 3.1 %collective-permute-start.1 = (s32[1,8]{1,0:T(1,128)}, s32[1,8]{1,0:T(1,128)S(1)}, u32[]{:S(2)}, u32[]{:S(2)}) collective-permute-start(s32[1,8]{1,0:T(1,128)} %param.9), channel_id=1, source_target_pairs={{0,8},{1,1},{2,510},{3,3},{4,12},{5,5},{6,506},{7,7},{8,0},{9,9},{... | collective-permute-start | bytes 104 | tf_op jit(solution)/shard_map/ppermute | solution.py:227
  17.4 9.2 %collective-permute-start.2 = (bf16[8,512]{1,0:T(8,128)(2,1)S(1)}, bf16[8,512]{1,0:T(8,128)(2,1)S(1)}, u32[]{:S(2)}, u32[]{:S(2)}) collective-permute-start(bf16[8,512]{1,0:T(8,128)(2,1)S(1)} %get-tuple-element.13), channel_id=1, source_target_pairs={{0,24},{1,493},{2,18},{3,503},{4,28},{5,489},{6,22},{7,499},{8,500... | collective-permute-start | bytes 24584 | tf_op jit(solution)/shard_map/ppermute | solution.py:233
  23.6 3.0 %collective-permute-start.3 = (bf16[8,512]{1,0:T(8,128)(2,1)S(1)}, bf16[8,512]{1,0:T(8,128)(2,1)S(1)}, u32[]{:S(2)}, u32[]{:S(2)}) collective-permute-start(bf16[8,512]{1,0:T(8,128)(2,1)S(1)} %get-tuple-element.14), channel_id=1, source_target_pairs={{0,8},{1,1},{2,510},{3,3},{4,12},{5,5},{6,506},{7,7},{8,0},{9,9},{... | collective-permute-start | bytes 24584 | tf_op jit(solution)/shard_map/ppermute | solution.py:233
  27.3 10.9 %all-to-all-start = ((bf16[4,2,8,512]{3,2,1,0:T(8,128)(2,1)}), bf16[4,2,8,512]{3,2,1,0:T(8,128)(2,1)S(1)}, u32[]{:S(2)}, u32[]{:S(2)}) async-start(bf16[4,2,8,512]{3,2,1,0:T(8,128)(2,1)} %broadcast_in_dim.2), calls=%async_computation | async-start | bytes 131072 | tf_op jit(solution)/shard_map/all_to_all | solution.py:222
  40.4 30.9 %all-to-all-start.1 = ((bf16[4,784,128]{2,1,0:T(8,128)(2,1)}), bf16[4,784,128]{2,1,0:T(8,128)(2,1)S(1)}, u32[]{:S(2)}, u32[]{:S(2)}) async-start(bf16[4,784,128]{2,1,0:T(8,128)(2,1)} %get-tuple-element.12), calls=%async_computation.1 | async-start | bytes 1605632 | tf_op jit(solution)/shard_map/all_to_all | solution.py:252
  45.3 26.0 %collective-permute-start.4 = (bf16[784,128]{1,0:T(8,128)(2,1)S(1)}, bf16[784,128]{1,0:T(8,128)(2,1)S(1)}, u32[]{:S(2)}, u32[]{:S(2)}) collective-permute-start(bf16[784,128]{1,0:T(8,128)(2,1)S(1)} %get-tuple-element.11.own_ref), channel_id=1, source_target_pairs={{0,4},{1,5},{2,6},{3,7},{4,0},{5,1},{6,2},{7,3},{8,12},{9,13},{10,... | collective-permute-start | bytes 602120 | tf_op jit(solution)/shard_map/ppermute | solution.py:251
  73.2 9.0 %all-to-all-start.2 = ((f32[4,32,128]{2,1,0:T(8,128)}), f32[4,32,128]{2,1,0:T(8,128)S(1)}, u32[]{:S(2)}, u32[]{:S(2)}) async-start(f32[4,32,128]{2,1,0:T(8,128)} %late.1), calls=%async_computation.2 | async-start | bytes 131072 | tf_op jit(solution)/shard_map/all_to_all | solution.py:269

commit v3 on v2

--- a/solution.py
+++ b/solution.py
@@ -19,7 +19,7 @@
 BF16 = jnp.bfloat16
 
 
-TASKS = (((3, 0), (3, 1), (2, 0), (2, 1)), ((1, 0), (0, 0), (1, 1), (0, 0)))
+TASKS = (((3, 0), (3, 1), (1, 1), (2, 1)), ((1, 0), (0, 0), (2, 0), (0, 0)))
 
 
 def swap_pairs(j, regions, zlo):
@@ -50,7 +50,8 @@
         phase = jnp.where(offset > 0, place, 1 - place)
         x = jnp.where(distance == 3, phase, jnp.where(distance == 0, 1, 2 * phase))
         x = jnp.where(distance == 2, 2 + phase, x)
-        j = jnp.where(distance > 1, 0, 1)
+        first = jnp.where(distance == 1, phase, jnp.where(distance == 2, phase, distance // 3))
+        j = 1 - first
         m = pattern_ref[0, 0, t, 1]
         lanes = pl.ds(pl.multiple_of((m // 2) * 128, 128), 128)
         part = window_ref[x, j, :, lanes].astype(F32)
@@ -108,67 +109,65 @@
     return [jnp.sum(jnp.where(lane == t, row, 0.0)).astype(jnp.int32) for t in range(NT)]
 
 
-def weights_of(metric_ref, rows, cols):
+NT_DIMS = (((1,), (1,)), ((), ()))
+
+
+def spread_lanes(block_ref, lead=()):
+    a_part = block_ref[lead + (slice(0, 512), slice(None))]
+    b_part = block_ref[lead + (slice(512, 768), slice(None))]
+    low = (lax.broadcasted_iota(jnp.int32, (1, 128), 1) < 64).astype(F32)
+    lo = jnp.concatenate([a_part[0:256], b_part * low.astype(BF16)], axis=1)
+    hi = jnp.concatenate([a_part[256:512], b_part * (1.0 - low).astype(BF16)], axis=1)
+    return jnp.concatenate([lo, hi], axis=0)
+
+
+def by_orbital(value):
+    return jnp.concatenate([value[i * BF : (i + 1) * BF] for i in range(OSUP)], axis=1)
+
+
+def tags_of(block_ref, lead=()):
+    return blocks_of(block_ref[lead + (slice(768, 784), slice(None))][0:1])
+
+
+def rows_of(columns_ref, rows, lanes):
+    return jnp.concatenate([columns_ref[p, :, lanes] for p in (rows[0], rows[1], rows[2], rows[2])], axis=0)
+
+
+def columns_kernel(window_ref, metric_ref, columns_ref):
     low = lax.broadcasted_iota(jnp.int32, (AB, 128), 1) < 64
-    zero = jnp.zeros((AB, 128), F32)
-
-    def piece(p, q, want_high):
-        part = metric_ref[p, :, pl.ds(pl.multiple_of((q // 2) * 128, 128), 128)].astype(F32)
-        return pltpu.roll(part, 64 * ((q % 2) ^ want_high), 1)
-
-    lo, hi = [], []
-    for p in rows:
-        first = jnp.where(low, piece(p, cols[0], 0), piece(p, cols[1], 1))
-        second = piece(p, cols[2], 0)
-        lo.append(jnp.concatenate([first, jnp.where(low, second, zero)], axis=1))
-        hi.append(jnp.concatenate([first, jnp.where(low, zero, pltpu.roll(second, 64, 1))], axis=1))
-    blank = jnp.zeros((AB, 256), F32)
-    lo = jnp.concatenate(lo + [blank], axis=0).astype(BF16)
-    hi = jnp.concatenate(hi[:2] + [blank, hi[2]], axis=0).astype(BF16)
-    return lo, hi
-
-
-def halves(a_part, b_part):
-    lo = jnp.concatenate([a_part[0:256], b_part], axis=1)
-    hi = jnp.concatenate([a_part[256:512], b_part], axis=1)
-    return lo, hi
-
-
-def by_orbital(lo, hi):
-    parts = [lo[i * 64 : (i + 1) * 64] for i in range(4)] + [hi[i * 64 : (i + 1) * 64] for i in range(4)]
-    return jnp.concatenate(parts, axis=1)
-
-
-def fitted_of(lo, hi, wlo, whi):
-    flo = jnp.dot(lo, wlo, preferred_element_type=F32).astype(BF16)
-    fhi = jnp.dot(hi, whi, preferred_element_type=F32).astype(BF16)
-    return by_orbital(flo, fhi)
-
-
-NT_DIMS = (((1,), (1,)), ((), ()))
-
-
-def early_kernel(own_ref, all_ref, metric_ref, out_ref):
-    cols = blocks_of(own_ref[768:784, :][0:1])
-    own = by_orbital(*halves(own_ref[0:512, :], own_ref[512:768, :]))
+    for x in range(XN):
+        cols = blocks_of(window_ref[x, 2, :, 0:128][0:1])
+        lanes = [pl.ds(pl.multiple_of((q // 2) * 128, 128), 128) for q in cols]
+        for p in range(AUXR // AB):
+            part = [metric_ref[p, :, lane].astype(F32) for lane in lanes]
+            first = pltpu.roll(part[0], 64 * (cols[0] % 2), 1)
+            second = pltpu.roll(part[1], 64 * (1 - cols[1] % 2), 1)
+            columns_ref[p, :, x * 256 : x * 256 + 128] = jnp.where(low, first, second).astype(BF16)
+            third = pltpu.roll(part[2], 64 * (cols[2] % 2), 1)
+            third = jnp.where(low, third, pltpu.roll(third, 64, 1))
+            columns_ref[p, :, x * 256 + 128 : x * 256 + 256] = third.astype(BF16)
+
+
+def early_kernel(group_ref, all_ref, columns_ref, out_ref):
+    tags = [tags_of(all_ref, (x,)) for x in range(XN)]
+    me = group_ref[0] % XN
+    own = by_orbital(spread_lanes(all_ref, (me,)))
+    lanes = pl.ds(pl.multiple_of(me * 256, 256), 256)
     fitted = []
     for x in range(XN):
-        rows = blocks_of(all_ref[x, 768:784, :][0:1])
-        wlo, whi = weights_of(metric_ref, rows, cols)
-        lo, hi = halves(all_ref[x, 0:512, :], all_ref[x, 512:768, :])
-        fitted.append(fitted_of(lo, hi, wlo, whi))
+        weights = rows_of(columns_ref, tags[x], lanes)
+        rows = jnp.dot(spread_lanes(all_ref, (x,)), weights, preferred_element_type=F32)
+        fitted.append(by_orbital(rows.astype(BF16)))
     fitted = jnp.concatenate(fitted, axis=0)
     out_ref[...] = lax.dot_general(own, fitted, NT_DIMS, preferred_element_type=F32)
 
 
-def late_kernel(far_ref, all_ref, metric_ref, out_ref):
-    rows = blocks_of(far_ref[768:784, :][0:1])
-    lo, hi = halves(far_ref[0:512, :], far_ref[512:768, :])
+def late_kernel(far_ref, all_ref, columns_ref, out_ref):
+    weights = rows_of(columns_ref, tags_of(far_ref), slice(None))
+    rows = jnp.dot(spread_lanes(far_ref), weights, preferred_element_type=F32).astype(BF16)
     for x in range(XN):
-        cols = blocks_of(all_ref[x, 768:784, :][0:1])
-        wlo, whi = weights_of(metric_ref, rows, cols)
-        fitted = fitted_of(lo, hi, wlo, whi)
-        mine = by_orbital(*halves(all_ref[x, 0:512, :], all_ref[x, 512:768, :]))
+        fitted = by_orbital(rows[:, x * 256 : (x + 1) * 256])
+        mine = by_orbital(spread_lanes(all_ref, (x,)))
         block = lax.dot_general(mine, fitted, NT_DIMS, preferred_element_type=F32)
         out_ref[x] = jnp.concatenate([block[0:32], block[32:64]], axis=1)
 
@@ -195,6 +194,10 @@
     return pl.BlockSpec(memory_space=pltpu.VMEM)
 
 
+def in_hbm(value):
+    return pltpu.with_memory_space_constraint(value, pltpu.HBM)
+
+
 def in_vmem(value):
     return pltpu.with_memory_space_constraint(value, pltpu.VMEM)
 
@@ -207,7 +210,7 @@
         out_specs=[vmem()] * len(parts),
         scratch_shapes=[pltpu.SemaphoreType.DMA] * len(parts),
         compiler_params=pltpu.CompilerParams(vmem_limit_bytes=16 * 2**20),
-    )(*[pltpu.with_memory_space_constraint(p, pltpu.HBM) for p in parts])
+    )(*[in_hbm(p) for p in parts])
 
 
 def per_device(occupied, integrals, metric_inv, pattern, support):
@@ -225,15 +228,18 @@
     asked = []
     for j in range(2):
         asked.append(lax.ppermute(support, axes, pairs[j]))
-    occupied, integrals = staged([occupied, integrals])
+    (occupied,) = staged([occupied])
+    (integrals,) = staged([integrals])
     asked = jnp.concatenate(asked, axis=1)[0]
     wanted = asked[:, None] == jnp.arange(occupied.shape[1], dtype=jnp.int32)[None, :]
     answer = lax.dot_general(wanted.astype(BF16), occupied, NT_DIMS, preferred_element_type=F32)
     answer = answer.astype(BF16)
-    answer = [lax.ppermute(answer[j * OSUP : (j + 1) * OSUP], axes, pairs[j]) for j in range(2)]
-    window = spread(jnp.stack(answer, 0))
-    (metric,) = staged([metric_inv])
-    metric = in_vmem(metric.reshape(AUXR // AB, AB, AUXR))
+    answers = []
+    for j in range(2):
+        answers.append(lax.ppermute(answer[j * OSUP : (j + 1) * OSUP], axes, pairs[j]))
+    tag = jnp.pad(pattern[0, 0, :, 2].astype(BF16), (0, occupied.shape[0] - NT))
+    answers.append(jnp.broadcast_to(tag, (OSUP, occupied.shape[0])))
+    window = spread(jnp.stack(answers, 0))
 
     message, copies = pl.pallas_call(
         contribution_kernel,
@@ -250,22 +256,31 @@
 
     far = lax.ppermute(message, "grp", [(g, (g + XN) % (2 * XN)) for g in range(2 * XN)])
     everyone = lax.all_to_all(copies, "grp", 0, 0, axis_index_groups=groups)
+    limit = pltpu.CompilerParams(vmem_limit_bytes=24 * 2**20)
+    columns = pl.pallas_call(
+        columns_kernel,
+        out_shape=pltpu.VMEM((AUXR // AB, AB, XN * 256), BF16),
+        in_specs=[vmem(), vmem()],
+        out_specs=vmem(),
+        compiler_params=limit,
+        name="columns",
+    )(in_vmem(window), in_hbm(metric_inv.reshape(AUXR // AB, AB, AUXR)))
     early = pl.pallas_call(
         early_kernel,
-        out_shape=jax.ShapeDtypeStruct((BF, XN * BF), F32),
+        out_shape=pltpu.VMEM((BF, XN * BF), F32),
+        in_specs=[smem(), vmem(), vmem()],
+        out_specs=vmem(),
+        compiler_params=limit,
+        name="early",
+    )(group, in_vmem(everyone), in_vmem(columns))
+    late = pl.pallas_call(
+        late_kernel,
+        out_shape=pltpu.VMEM((XN, BF // 2, 2 * BF), F32),
         in_specs=[vmem(), vmem(), vmem()],
         out_specs=vmem(),
-        name="early",
-        compiler_params=pltpu.CompilerParams(vmem_limit_bytes=16 * 2**20),
-    )(in_vmem(message), in_vmem(everyone), metric)
-    late = pl.pallas_call(
-        late_kernel,
-        out_shape=jax.ShapeDtypeStruct((XN, BF // 2, 2 * BF), F32),
-        in_specs=[vmem(), vmem(), vmem()],
-        out_specs=vmem(),
+        compiler_params=limit,
         name="late",
-            compiler_params=pltpu.CompilerParams(vmem_limit_bytes=16 * 2**20),
-    )(in_vmem(far), in_vmem(everyone), metric)
+    )(in_vmem(far), in_vmem(everyone), in_vmem(columns))
     late = lax.all_to_all(late, "grp", 0, 0, axis_index_groups=groups)
     return pl.pallas_call(
         join_kernel,
@@ -274,7 +289,7 @@
         out_specs=vmem(),
         name="join",
             compiler_params=pltpu.CompilerParams(vmem_limit_bytes=16 * 2**20),
-    )(group, early, in_vmem(late))
+    )(group, in_vmem(early), in_vmem(late))
 
 
 def solution(mesh):

time: 83.4 us -> 83.7 us (level)
  the two profiles are of different devices: /device:TPU:2 before, /device:TPU:1 now
where the time goes in v3:
time: 83.7 us; the launch traced here: 83.1 us
  starting transfers between devices  44 us (53%)
  waiting for transfers between devices  22.5 us (27%)
  Pallas kernels  15.1 us (18%)
    ppermute x2, starting transfers between devices, per_device(): asked.append(lax.ppermute(support, axes, pairs[j]))  17 us
    ppermute x1, waiting for transfers between devices, per_device(): lax.ppermute(message, 'grp', [(g, (g + XN) % (2 * XN)) for g in range(2 *...  15.2 us
    ppermute x2, starting transfers between devices, per_device(): lax.ppermute(answer[j * OSUP:(j + 1) * OSUP], axes, pairs[j])  8.89 us
    ppermute x1, starting transfers between devices, per_device(): lax.ppermute(message, 'grp', [(g, (g + XN) % (2 * XN)) for g in range(2 *...  7.19 us
    pallas_call x1, Pallas kernels, per_device(): pl.pallas_call(columns_kernel, out_shape=pltpu.VMEM((AUXR // AB, AB, XN *...  6.63 us
    all_to_all x1, starting transfers between devices, per_device(): late = lax.all_to_all(late, 'grp', 0, 0, axis_index_groups=groups)  4.18 us
    all_to_all x1, starting transfers between devices, per_device(): everyone = lax.all_to_all(copies, 'grp', 0, 0, axis_index_groups=groups)  3.49 us
    all_to_all x1, starting transfers between devices, spread(): return lax.all_to_all(value, 'grp', 0, 0, axis_index_groups=groups)  3.3 us
  transfers between devices with their start and end apart: 8, of which 5 were waited for; matrix products, arithmetic and copies ran while one was open for 0% of the time, Pallas kernels for 13%

profile of v3, /device:TPU:1, one launch (start us, length us, event | category | flops | bytes accessed | tf_op | source)
XLA Modules:
  0.0 83.1 jit_solution(630927325039110223)
XLA Ops:
  0.0 8.9 %collective-permute-start.1 = (s32[1,8]{1,0:T(1,128)}, s32[1,8]{1,0:T(1,128)S(1)}, u32[]{:S(2)}, u32[]{:S(2)}) collective-permute-start(s32[1,8]{1,0:T(1,128)} %param.9), channel_id=1, source_target_pairs={{0,8},{1,1},{2,18},{3,3},{4,12},{5,5},{6,22},{7,7},{8,0},{9,9},{10... | collective-permute-start | bytes 104 | tf_op jit(solution)/shard_map/ppermute | solution.py:230
  8.9 8.1 %collective-permute-start = (s32[1,8]{1,0:T(1,128)}, s32[1,8]{1,0:T(1,128)S(1)}, u32[]{:S(2)}, u32[]{:S(2)}) collective-permute-start(s32[1,8]{1,0:T(1,128)} %param.9), channel_id=1, source_target_pairs={{0,24},{1,493},{2,510},{3,503},{4,28},{5,489},{6,506},{7,499},{8,5... | collective-permute-start | bytes 104 | tf_op jit(solution)/shard_map/ppermute | solution.py:230
  17.0 1.2 %shard_map.55 = bf16[512,1024]{1,0:T(8,128)(2,1)S(1)} custom-call(bf16[512,1024]{1,0:T(8,128)(2,1)} %refs_0_.2), custom_call_target="tpu_custom_call" | custom-call | tf_op jit(solution)/shard_map/pallas_call | solution.py:206
  18.3 0.1 collective-permute-done
  18.4 0.1 add_bitcast_fusion
  18.5 0.4 convolution_convert_fusion
  18.8 7.0 %collective-permute-start.2 = (bf16[8,512]{1,0:T(8,128)(2,1)S(1)}, bf16[8,512]{1,0:T(8,128)(2,1)S(1)}, u32[]{:S(2)}, u32[]{:S(2)}) collective-permute-start(bf16[8,512]{1,0:T(8,128)(2,1)S(1)} %get-tuple-element.9), channel_id=1, source_target_pairs={{0,24},{1,493},{2,510},{3,503},{4,28},{5,489},{6,506},{7,499},{8,5... | collective-permute-start | bytes 24584 | tf_op jit(solution)/shard_map/ppermute | solution.py:239
  25.8 1.9 %collective-permute-start.3 = (bf16[8,512]{1,0:T(8,128)(2,1)S(1)}, bf16[8,512]{1,0:T(8,128)(2,1)S(1)}, u32[]{:S(2)}, u32[]{:S(2)}) collective-permute-start(bf16[8,512]{1,0:T(8,128)(2,1)S(1)} %get-tuple-element.10), channel_id=1, source_target_pairs={{0,8},{1,1},{2,18},{3,3},{4,12},{5,5},{6,22},{7,7},{8,0},{9,9},{10... | collective-permute-start | bytes 24584 | tf_op jit(solution)/shard_map/ppermute | solution.py:239
  27.8 0.2 fusion.1
  27.9 0.9 %collective-permute-done.3 = bf16[8,512]{1,0:T(8,128)(2,1)S(1)} collective-permute-done((bf16[8,512]{1,0:T(8,128)(2,1)S(1)}, bf16[8,512]{1,0:T(8,128)(2,1)S(1)}, u32[]{:S(2)}, u32[]{:S(2)}) %collective-permute-start.3) | collective-permute-done | bytes 8224 | tf_op jit(solution)/shard_map/ppermute | solution.py:239
  28.9 0.7 broadcast_in_dim.2
  29.5 3.3 %all-to-all-start = ((bf16[4,3,8,512]{3,2,1,0:T(8,128)(2,1)}), bf16[4,3,8,512]{3,2,1,0:T(8,128)(2,1)S(1)}, u32[]{:S(2)}, u32[]{:S(2)}) async-start(bf16[4,3,8,512]{3,2,1,0:T(8,128)(2,1)} %broadcast_in_dim.2), calls=%async_computation | async-start | bytes 196608 | tf_op jit(solution)/shard_map/all_to_all | solution.py:225
  32.9 1.4 %shard_map.56.integrals_ref = bf16[1,1,3,64,4096]{4,3,2,1,0:T(8,128)(2,1)S(1)} custom-call(bf16[1,1,3,64,4096]{4,3,2,1,0:T(8,128)(2,1)} %refs_0_.3), custom_call_target="tpu_custom_call" | custom-call | tf_op jit(solution)/shard_map/pallas_call | solution.py:206
  34.3 3.2 %all-to-all-done.window_ref = bf16[4,3,8,512]{3,2,1,0:T(8,128)(2,1)S(1)} async-done(((bf16[4,3,8,512]{3,2,1,0:T(8,128)(2,1)}), bf16[4,3,8,512]{3,2,1,0:T(8,128)(2,1)S(1)}, u32[]{:S(2)}, u32[]{:S(2)}) %all-to-all-start) | async-done | bytes 98336 | tf_op jit(solution)/shard_map/all_to_all | solution.py:225
  37.5 2.2 %contribution.1 = (bf16[784,128]{1,0:T(8,128)(2,1)S(1)}, bf16[4,784,128]{2,1,0:T(8,128)(2,1)}) custom-call(s32[1]{0:T(128)} %bitcast.1.region_ref, s32[1,1,3,4]{3,2,1,0:T(4,128)S(1)} %copy.7.pattern_ref, bf16[4,3,8,512]{3,2,1,0:T(8,128)(2,1)S(1)} %all-to-all-done.window_ref, bf16[1,1,3,64,4096]{4,3,2,1,0:T(8,128)(2,1)S(1)} %shard_map.56.integrals_ref), custom_call_target="tpu_custom_call" | custom-call | tf_op jit(solution)/shard_map/contribution/pallas_call | solution.py:244
  39.7 3.5 %all-to-all-start.1 = ((bf16[4,784,128]{2,1,0:T(8,128)(2,1)}), bf16[4,784,128]{2,1,0:T(8,128)(2,1)S(1)}, u32[]{:S(2)}, u32[]{:S(2)}) async-start(bf16[4,784,128]{2,1,0:T(8,128)(2,1)} %get-tuple-element.7), calls=%async_computation.1 | async-start | bytes 1605632 | tf_op jit(solution)/shard_map/all_to_all | solution.py:258
  43.2 7.2 %collective-permute-start.4 = (bf16[784,128]{1,0:T(8,128)(2,1)S(1)}, bf16[784,128]{1,0:T(8,128)(2,1)S(1)}, u32[]{:S(2)}, u32[]{:S(2)}) collective-permute-start(bf16[784,128]{1,0:T(8,128)(2,1)S(1)} %get-tuple-element.8), channel_id=1, source_target_pairs={{0,4},{1,5},{2,6},{3,7},{4,0},{5,1},{6,2},{7,3},{8,12},{9,13},{10,... | collective-permute-start | bytes 602120 | tf_op jit(solution)/shard_map/ppermute | solution.py:257
  50.4 6.6 %columns.1.columns_ref = bf16[16,64,1024]{2,1,0:T(8,128)(2,1)S(1)} custom-call(bf16[4,3,8,512]{3,2,1,0:T(8,128)(2,1)S(1)} %all-to-all-done.window_ref, bf16[16,64,1024]{2,1,0:T(8,128)(2,1)} %bitcast.8), custom_call_target="tpu_custom_call" | custom-call | tf_op jit(solution)/shard_map/columns/pallas_call | solution.py:260
  57.0 15.2 %collective-permute-done.4.far_ref = bf16[784,128]{1,0:T(8,128)(2,1)S(1)} collective-permute-done((bf16[784,128]{1,0:T(8,128)(2,1)S(1)}, bf16[784,128]{1,0:T(8,128)(2,1)S(1)}, u32[]{:S(2)}, u32[]{:S(2)}) %collective-permute-start.4) | collective-permute-done | bytes 200736 | tf_op jit(solution)/shard_map/ppermute | solution.py:257
  72.2 1.5 %late.1 = f32[4,32,128]{2,1,0:T(8,128)} custom-call(bf16[784,128]{1,0:T(8,128)(2,1)S(1)} %collective-permute-done.4.far_ref, bf16[4,784,128]{2,1,0:T(8,128)(2,1)S(1)} %all-to-all-done.1.all_ref, bf16[16,64,1024]{2,1,0:T(8,128)(2,1)S(1)} %columns.1.columns_ref), custom_call_target="tpu_custom_call" | custom-call | tf_op jit(solution)/shard_map/late/pallas_call | solution.py:276
  73.7 4.2 %all-to-all-start.2 = ((f32[4,32,128]{2,1,0:T(8,128)}), f32[4,32,128]{2,1,0:T(8,128)S(1)}, u32[]{:S(2)}, u32[]{:S(2)}) async-start(f32[4,32,128]{2,1,0:T(8,128)} %late.1), calls=%async_computation.2 | async-start | bytes 131072 | tf_op jit(solution)/shard_map/all_to_all | solution.py:284
  77.9 1.4 %early.1.early_ref = f32[64,256]{1,0:T(8,128)S(1)} custom-call(s32[1]{0:T(128)} %bitcast.group_ref, bf16[4,784,128]{2,1,0:T(8,128)(2,1)S(1)} %all-to-all-done.1.all_ref, bf16[16,64,1024]{2,1,0:T(8,128)(2,1)S(1)} %columns.1.columns_ref), custom_call_target="tpu_custom_call" | custom-call | tf_op jit(solution)/shard_map/early/pallas_call | solution.py:268
  79.3 3.1 %all-to-all-done.2.late_ref = f32[4,32,128]{2,1,0:T(8,128)S(1)} async-done(((f32[4,32,128]{2,1,0:T(8,128)}), f32[4,32,128]{2,1,0:T(8,128)S(1)}, u32[]{:S(2)}, u32[]{:S(2)}) %all-to-all-start.2) | async-done | bytes 65568 | tf_op jit(solution)/shard_map/all_to_all | solution.py:284
  82.4 0.7 join.1
  (10 shorter events, 0.0 us)
Async XLA Ops:
  0.0 27.7 %copy-start = (s32[1,1,3,4]{3,1,2,0:T(1,128)S(1)}, s32[1,1,3,4]{3,1,2,0:T(1,128)}, u32[]{:S(2)}) copy-start(s32[1,1,3,4]{3,1,2,0:T(1,128)} %param.8) | copy-start | bytes 148
  0.0 18.3 %collective-permute-start.1 = (s32[1,8]{1,0:T(1,128)}, s32[1,8]{1,0:T(1,128)S(1)}, u32[]{:S(2)}, u32[]{:S(2)}) collective-permute-start(s32[1,8]{1,0:T(1,128)} %param.9), channel_id=1, source_target_pairs={{0,8},{1,1},{2,18},{3,3},{4,12},{5,5},{6,22},{7,7},{8,0},{9,9},{10... | collective-permute-start | bytes 104 | tf_op jit(solution)/shard_map/ppermute | solution.py:230
  8.9 9.5 %collective-permute-start = (s32[1,8]{1,0:T(1,128)}, s32[1,8]{1,0:T(1,128)S(1)}, u32[]{:S(2)}, u32[]{:S(2)}) collective-permute-start(s32[1,8]{1,0:T(1,128)} %param.9), channel_id=1, source_target_pairs={{0,24},{1,493},{2,510},{3,503},{4,28},{5,489},{6,506},{7,499},{8,5... | collective-permute-start | bytes 104 | tf_op jit(solution)/shard_map/ppermute | solution.py:230
  18.8 9.1 %collective-permute-start.2 = (bf16[8,512]{1,0:T(8,128)(2,1)S(1)}, bf16[8,512]{1,0:T(8,128)(2,1)S(1)}, u32[]{:S(2)}, u32[]{:S(2)}) collective-permute-start(bf16[8,512]{1,0:T(8,128)(2,1)S(1)} %get-tuple-element.9), channel_id=1, source_target_pairs={{0,24},{1,493},{2,510},{3,503},{4,28},{5,489},{6,506},{7,499},{8,5... | collective-permute-start | bytes 24584 | tf_op jit(solution)/shard_map/ppermute | solution.py:239
  25.8 3.1 %collective-permute-start.3 = (bf16[8,512]{1,0:T(8,128)(2,1)S(1)}, bf16[8,512]{1,0:T(8,128)(2,1)S(1)}, u32[]{:S(2)}, u32[]{:S(2)}) collective-permute-start(bf16[8,512]{1,0:T(8,128)(2,1)S(1)} %get-tuple-element.10), channel_id=1, source_target_pairs={{0,8},{1,1},{2,18},{3,3},{4,12},{5,5},{6,22},{7,7},{8,0},{9,9},{10... | collective-permute-start | bytes 24584 | tf_op jit(solution)/shard_map/ppermute | solution.py:239
  29.5 7.9 %all-to-all-start = ((bf16[4,3,8,512]{3,2,1,0:T(8,128)(2,1)}), bf16[4,3,8,512]{3,2,1,0:T(8,128)(2,1)S(1)}, u32[]{:S(2)}, u32[]{:S(2)}) async-start(bf16[4,3,8,512]{3,2,1,0:T(8,128)(2,1)} %broadcast_in_dim.2), calls=%async_computation | async-start | bytes 196608 | tf_op jit(solution)/shard_map/all_to_all | solution.py:225
  39.7 32.5 %all-to-all-start.1 = ((bf16[4,784,128]{2,1,0:T(8,128)(2,1)}), bf16[4,784,128]{2,1,0:T(8,128)(2,1)S(1)}, u32[]{:S(2)}, u32[]{:S(2)}) async-start(bf16[4,784,128]{2,1,0:T(8,128)(2,1)} %get-tuple-element.7), calls=%async_computation.1 | async-start | bytes 1605632 | tf_op jit(solution)/shard_map/all_to_all | solution.py:258
  43.2 29.0 %collective-permute-start.4 = (bf16[784,128]{1,0:T(8,128)(2,1)S(1)}, bf16[784,128]{1,0:T(8,128)(2,1)S(1)}, u32[]{:S(2)}, u32[]{:S(2)}) collective-permute-start(bf16[784,128]{1,0:T(8,128)(2,1)S(1)} %get-tuple-element.8), channel_id=1, source_target_pairs={{0,4},{1,5},{2,6},{3,7},{4,0},{5,1},{6,2},{7,3},{8,12},{9,13},{10,... | collective-permute-start | bytes 602120 | tf_op jit(solution)/shard_map/ppermute | solution.py:257
  73.7 8.7 %all-to-all-start.2 = ((f32[4,32,128]{2,1,0:T(8,128)}), f32[4,32,128]{2,1,0:T(8,128)S(1)}, u32[]{:S(2)}, u32[]{:S(2)}) async-start(f32[4,32,128]{2,1,0:T(8,128)} %late.1), calls=%async_computation.2 | async-start | bytes 131072 | tf_op jit(solution)/shard_map/all_to_all | solution.py:284

commit v4 on v3

--- a/solution.py
+++ b/solution.py
@@ -35,15 +35,15 @@
     return pairs
 
 
-def contribution_kernel(region_ref, pattern_ref, window_ref, integrals_ref, out_ref, all_ref, sa_ref, sb_ref):
+def contribution_kernel(region_ref, pattern_ref, window_ref, integrals_ref, out_ref, sa_ref, sb_ref):
     region = region_ref[0]
-    a = [pattern_ref[0, 0, t, 2] for t in range(NT)]
-    live = [pattern_ref[0, 0, t, 3] for t in range(NT)]
+    a = [pattern_ref[4 * t + 2] for t in range(NT)]
+    live = [pattern_ref[4 * t + 3] for t in range(NT)]
     lane8 = lax.broadcasted_iota(jnp.int32, (OSUP, 128), 1)
     low8 = lane8 < 64
 
     def tile(t, want_high):
-        source = pattern_ref[0, 0, t, 0]
+        source = pattern_ref[4 * t + 0]
         offset = (source - region + 64 + REACH) % 64 - REACH
         distance = jnp.abs(offset)
         place = jnp.where(distance == 2, region // 2, region) % 2
@@ -52,7 +52,7 @@
         x = jnp.where(distance == 2, 2 + phase, x)
         first = jnp.where(distance == 1, phase, jnp.where(distance == 2, phase, distance // 3))
         j = 1 - first
-        m = pattern_ref[0, 0, t, 1]
+        m = pattern_ref[4 * t + 1]
         lanes = pl.ds(pl.multiple_of((m // 2) * 128, 128), 128)
         part = window_ref[x, j, :, lanes].astype(F32)
         return pltpu.roll(part, 64 * ((m % 2) ^ want_high), 1)
@@ -86,10 +86,6 @@
     out_ref[0:512, :] = a_part
     out_ref[512:768, :] = b_part
     out_ref[768:784, :] = tag
-    for copy in range(XN):
-        all_ref[copy, 0:512, :] = a_part
-        all_ref[copy, 512:768, :] = b_part
-        all_ref[copy, 768:784, :] = tag
 
 
 def stage_kernel(*refs):
@@ -239,23 +235,21 @@
         answers.append(lax.ppermute(answer[j * OSUP : (j + 1) * OSUP], axes, pairs[j]))
     tag = jnp.pad(pattern[0, 0, :, 2].astype(BF16), (0, occupied.shape[0] - NT))
     answers.append(jnp.broadcast_to(tag, (OSUP, occupied.shape[0])))
-    window = spread(jnp.stack(answers, 0))
-
-    message, copies = pl.pallas_call(
+    stacked, slots, region = lax.optimization_barrier((jnp.stack(answers, 0), pattern.reshape(-1), region))
+    window = spread(stacked)
+
+    message = pl.pallas_call(
         contribution_kernel,
-        out_shape=[
-            pltpu.VMEM((ROWS, 128), BF16),
-            jax.ShapeDtypeStruct((XN, ROWS, 128), BF16),
-        ],
+        out_shape=pltpu.VMEM((ROWS, 128), BF16),
         in_specs=[smem(), smem(), vmem(), vmem()],
-        out_specs=[vmem(), vmem()],
+        out_specs=vmem(),
         scratch_shapes=[pltpu.VMEM((512, 128), F32), pltpu.VMEM((256, 128), F32)],
         name="contribution",
             compiler_params=pltpu.CompilerParams(vmem_limit_bytes=16 * 2**20),
-    )(region, pattern, in_vmem(window), in_vmem(integrals))
+    )(region, slots, in_vmem(window), in_vmem(integrals))
 
     far = lax.ppermute(message, "grp", [(g, (g + XN) % (2 * XN)) for g in range(2 * XN)])
-    everyone = lax.all_to_all(copies, "grp", 0, 0, axis_index_groups=groups)
+    everyone = spread(message)
     limit = pltpu.CompilerParams(vmem_limit_bytes=24 * 2**20)
     columns = pl.pallas_call(
         columns_kernel,
@@ -300,6 +294,4 @@
         P("blk", "grp", None, None),
         P("blk", None),
     )
-    return jax.shard_map(
-        per_device, mesh=mesh, in_specs=placed, out_specs=P(("blk", "grp"), None), check_vma=False
-    )
+    return jax.shard_map(per_device, mesh=mesh, in_specs=placed, out_specs=P(("blk", "grp"), None), check_vma=False)

time: 83.7 us -> 83.7 us (level)
  local copies, waits for them, and re-layouts: 0.67 us -> 1.75 us
  Pallas kernels: 15.1 us -> 14.2 us
    all_to_all x1 -> x2, starting transfers between devices: 3.3 us -> 6.8 us  [spread(): return lax.all_to_all(value, 'grp', 0, 0, axis_index_groups=groups)]
    all_to_all x1 -> x0, starting transfers between devices: 3.49 us -> none  [per_device(): everyone = lax.all_to_all(copies, 'grp', 0, 0, axis_index_groups=groups)]
    broadcast_in_dim x1 -> x2, local copies, waits for them, and re-layouts: 0.65 us -> 1.65 us  [spread(): value = jnp.broadcast_to(value[None], (XN,) + value.shape)]
    pallas_call x1, Pallas kernels: 2.19 us -> 1.22 us  [per_device(): pl.pallas_call(contribution_kernel, out_shape=pltpu.VMEM((ROWS, 128), BF1...]
    all_to_all x1 -> x2, waiting for transfers between devices: 3.17 us -> 3.19 us  [spread(): return lax.all_to_all(value, 'grp', 0, 0, axis_index_groups=groups)]
where the time goes in v4:
time: 83.7 us; the launch traced here: 83.1 us
  starting transfers between devices  44 us (53%)
  waiting for transfers between devices  22.4 us (27%)
  Pallas kernels  14.2 us (17%)
  local copies, waits for them, and re-layouts  1.75 us (2%)
    ppermute x2, starting transfers between devices, per_device(): asked.append(lax.ppermute(support, axes, pairs[j]))  17 us
    ppermute x1, waiting for transfers between devices, per_device(): lax.ppermute(message, 'grp', [(g, (g + XN) % (2 * XN)) for g in range(2 *...  15.2 us
    ppermute x2, starting transfers between devices, per_device(): lax.ppermute(answer[j * OSUP:(j + 1) * OSUP], axes, pairs[j])  8.89 us
    ppermute x1, starting transfers between devices, per_device(): lax.ppermute(message, 'grp', [(g, (g + XN) % (2 * XN)) for g in range(2 *...  7.19 us
    all_to_all x2, starting transfers between devices, spread(): return lax.all_to_all(value, 'grp', 0, 0, axis_index_groups=groups)  6.8 us
    pallas_call x1, Pallas kernels, per_device(): pl.pallas_call(columns_kernel, out_shape=pltpu.VMEM((AUXR // AB, AB, XN *...  6.63 us
    all_to_all x1, starting transfers between devices, per_device(): late = lax.all_to_all(late, 'grp', 0, 0, axis_index_groups=groups)  4.18 us
    all_to_all x2, waiting for transfers between devices, spread(): return lax.all_to_all(value, 'grp', 0, 0, axis_index_groups=groups)  3.19 us
  transfers between devices with their start and end apart: 8, of which 5 were waited for; matrix products, arithmetic and copies ran while one was open for 0% of the time, Pallas kernels for 13%

profile of v4, /device:TPU:1, one launch (start us, length us, event | category | flops | bytes accessed | tf_op | source)
XLA Modules:
  0.0 83.1 jit_solution(16197422269142196499)
XLA Ops:
  0.0 8.9 %collective-permute-start.1 = (s32[1,8]{1,0:T(1,128)}, s32[1,8]{1,0:T(1,128)S(1)}, u32[]{:S(2)}, u32[]{:S(2)}) collective-permute-start(s32[1,8]{1,0:T(1,128)} %param.9), channel_id=1, source_target_pairs={{0,8},{1,1},{2,18},{3,3},{4,12},{5,5},{6,22},{7,7},{8,0},{9,9},{10... | collective-permute-start | bytes 104 | tf_op jit(solution)/shard_map/ppermute | solution.py:226
  8.9 8.1 %collective-permute-start = (s32[1,8]{1,0:T(1,128)}, s32[1,8]{1,0:T(1,128)S(1)}, u32[]{:S(2)}, u32[]{:S(2)}) collective-permute-start(s32[1,8]{1,0:T(1,128)} %param.9), channel_id=1, source_target_pairs={{0,24},{1,493},{2,510},{3,503},{4,28},{5,489},{6,506},{7,499},{8,5... | collective-permute-start | bytes 104 | tf_op jit(solution)/shard_map/ppermute | solution.py:226
  17.0 1.2 %shard_map.55 = bf16[512,1024]{1,0:T(8,128)(2,1)S(1)} custom-call(bf16[512,1024]{1,0:T(8,128)(2,1)} %refs_0_.2), custom_call_target="tpu_custom_call" | custom-call | tf_op jit(solution)/shard_map/pallas_call | solution.py:202
  18.3 0.1 collective-permute-done
  18.5 0.4 convolution_convert_fusion
  18.8 7.0 %collective-permute-start.2 = (bf16[8,512]{1,0:T(8,128)(2,1)S(1)}, bf16[8,512]{1,0:T(8,128)(2,1)S(1)}, u32[]{:S(2)}, u32[]{:S(2)}) collective-permute-start(bf16[8,512]{1,0:T(8,128)(2,1)S(1)} %get-tuple-element.11), channel_id=1, source_target_pairs={{0,24},{1,493},{2,510},{3,503},{4,28},{5,489},{6,506},{7,499},{8,5... | collective-permute-start | bytes 24584 | tf_op jit(solution)/shard_map/ppermute | solution.py:235
  25.8 1.9 %collective-permute-start.3 = (bf16[8,512]{1,0:T(8,128)(2,1)S(1)}, bf16[8,512]{1,0:T(8,128)(2,1)S(1)}, u32[]{:S(2)}, u32[]{:S(2)}) collective-permute-start(bf16[8,512]{1,0:T(8,128)(2,1)S(1)} %get-tuple-element.12), channel_id=1, source_target_pairs={{0,8},{1,1},{2,18},{3,3},{4,12},{5,5},{6,22},{7,7},{8,0},{9,9},{10... | collective-permute-start | bytes 24584 | tf_op jit(solution)/shard_map/ppermute | solution.py:235
  27.8 0.2 fusion.1
  28.0 0.8 %collective-permute-done.3 = bf16[8,512]{1,0:T(8,128)(2,1)S(1)} collective-permute-done((bf16[8,512]{1,0:T(8,128)(2,1)S(1)}, bf16[8,512]{1,0:T(8,128)(2,1)S(1)}, u32[]{:S(2)}, u32[]{:S(2)}) %collective-permute-start.3) | collective-permute-done | bytes 8224 | tf_op jit(solution)/shard_map/ppermute | solution.py:235
  28.9 0.7 broadcast_in_dim.4
  29.5 3.3 %all-to-all-start = ((bf16[4,3,8,512]{3,2,1,0:T(8,128)(2,1)}), bf16[4,3,8,512]{3,2,1,0:T(8,128)(2,1)S(1)}, u32[]{:S(2)}, u32[]{:S(2)}) async-start(bf16[4,3,8,512]{3,2,1,0:T(8,128)(2,1)} %broadcast_in_dim.4), calls=%async_computation | async-start | bytes 196608 | tf_op jit(solution)/shard_map/all_to_all | solution.py:221
  32.9 1.4 %shard_map.56.integrals_ref = bf16[1,1,3,64,4096]{4,3,2,1,0:T(8,128)(2,1)S(1)} custom-call(bf16[1,1,3,64,4096]{4,3,2,1,0:T(8,128)(2,1)} %refs_0_.3), custom_call_target="tpu_custom_call" | custom-call | tf_op jit(solution)/shard_map/pallas_call | solution.py:202
  34.3 3.2 %all-to-all-done.window_ref = bf16[4,3,8,512]{3,2,1,0:T(8,128)(2,1)S(1)} async-done(((bf16[4,3,8,512]{3,2,1,0:T(8,128)(2,1)}), bf16[4,3,8,512]{3,2,1,0:T(8,128)(2,1)S(1)}, u32[]{:S(2)}, u32[]{:S(2)}) %all-to-all-start) | async-done | bytes 98336 | tf_op jit(solution)/shard_map/all_to_all | solution.py:221
  37.5 1.2 %contribution.1 = bf16[784,128]{1,0:T(8,128)(2,1)S(1)} custom-call(s32[1]{0:T(128)} %bitcast.4.region_ref, s32[12]{0:T(128)S(1)} %reshape.17.pattern_ref, bf16[4,3,8,512]{3,2,1,0:T(8,128)(2,1)S(1)} %all-to-all-done.window_ref, bf16[1,1,3,64,4096]{4,3,2,1,0:T(8,128)(2,1)S(1)} %shard_map.56.integrals_ref), custom_call_target="tpu_custom_call" | custom-call | tf_op jit(solution)/shard_map/contribution/pallas_call | solution.py:241
  38.7 1.0 %broadcast_in_dim.5 = bf16[4,784,128]{2,1,0:T(8,128)(2,1)} broadcast(bf16[784,128]{1,0:T(8,128)(2,1)S(1)} %contribution.1), dimensions={1,2} | broadcast | bytes 1003520 | tf_op jit(solution)/shard_map/broadcast_in_dim | solution.py:220
  39.7 3.5 %all-to-all-start.1 = ((bf16[4,784,128]{2,1,0:T(8,128)(2,1)}), bf16[4,784,128]{2,1,0:T(8,128)(2,1)S(1)}, u32[]{:S(2)}, u32[]{:S(2)}) async-start(bf16[4,784,128]{2,1,0:T(8,128)(2,1)} %broadcast_in_dim.5), calls=%async_computation.1 | async-start | bytes 1605632 | tf_op jit(solution)/shard_map/all_to_all | solution.py:221
  43.2 7.2 %collective-permute-start.4 = (bf16[784,128]{1,0:T(8,128)(2,1)S(1)}, bf16[784,128]{1,0:T(8,128)(2,1)S(1)}, u32[]{:S(2)}, u32[]{:S(2)}) collective-permute-start(bf16[784,128]{1,0:T(8,128)(2,1)S(1)} %contribution.1), channel_id=1, source_target_pairs={{0,4},{1,5},{2,6},{3,7},{4,0},{5,1},{6,2},{7,3},{8,12},{9,13},{10,... | collective-permute-start | bytes 602120 | tf_op jit(solution)/shard_map/ppermute | solution.py:251
  50.4 6.6 %columns.1.columns_ref = bf16[16,64,1024]{2,1,0:T(8,128)(2,1)S(1)} custom-call(bf16[4,3,8,512]{3,2,1,0:T(8,128)(2,1)S(1)} %all-to-all-done.window_ref, bf16[16,64,1024]{2,1,0:T(8,128)(2,1)} %bitcast.8), custom_call_target="tpu_custom_call" | custom-call | tf_op jit(solution)/shard_map/columns/pallas_call | solution.py:254
  57.0 15.2 %collective-permute-done.4.far_ref = bf16[784,128]{1,0:T(8,128)(2,1)S(1)} collective-permute-done((bf16[784,128]{1,0:T(8,128)(2,1)S(1)}, bf16[784,128]{1,0:T(8,128)(2,1)S(1)}, u32[]{:S(2)}, u32[]{:S(2)}) %collective-permute-start.4) | collective-permute-done | bytes 200736 | tf_op jit(solution)/shard_map/ppermute | solution.py:251
  72.2 1.5 %late.1 = f32[4,32,128]{2,1,0:T(8,128)} custom-call(bf16[784,128]{1,0:T(8,128)(2,1)S(1)} %collective-permute-done.4.far_ref, bf16[4,784,128]{2,1,0:T(8,128)(2,1)S(1)} %all-to-all-done.1.all_ref, bf16[16,64,1024]{2,1,0:T(8,128)(2,1)S(1)} %columns.1.columns_ref), custom_call_target="tpu_custom_call" | custom-call | tf_op jit(solution)/shard_map/late/pallas_call | solution.py:270
  73.7 4.2 %all-to-all-start.2 = ((f32[4,32,128]{2,1,0:T(8,128)}), f32[4,32,128]{2,1,0:T(8,128)S(1)}, u32[]{:S(2)}, u32[]{:S(2)}) async-start(f32[4,32,128]{2,1,0:T(8,128)} %late.1), calls=%async_computation.2 | async-start | bytes 131072 | tf_op jit(solution)/shard_map/all_to_all | solution.py:278
  77.9 1.4 %early.1.early_ref = f32[64,256]{1,0:T(8,128)S(1)} custom-call(s32[1]{0:T(128)} %bitcast.group_ref, bf16[4,784,128]{2,1,0:T(8,128)(2,1)S(1)} %all-to-all-done.1.all_ref, bf16[16,64,1024]{2,1,0:T(8,128)(2,1)S(1)} %columns.1.columns_ref), custom_call_target="tpu_custom_call" | custom-call | tf_op jit(solution)/shard_map/early/pallas_call | solution.py:262
  79.3 3.1 %all-to-all-done.2.late_ref = f32[4,32,128]{2,1,0:T(8,128)S(1)} async-done(((f32[4,32,128]{2,1,0:T(8,128)}), f32[4,32,128]{2,1,0:T(8,128)S(1)}, u32[]{:S(2)}, u32[]{:S(2)}) %all-to-all-start.2) | async-done | bytes 65568 | tf_op jit(solution)/shard_map/all_to_all | solution.py:278
  82.4 0.7 join.1
  (12 shorter events, 0.2 us)
Async XLA Ops:
  0.0 27.7 %copy-start = (s32[1,1,3,4]{3,1,2,0:T(1,128)S(1)}, s32[1,1,3,4]{3,1,2,0:T(1,128)}, u32[]{:S(2)}) copy-start(s32[1,1,3,4]{3,1,2,0:T(1,128)} %param.8) | copy-start | bytes 148
  0.0 18.3 %collective-permute-start.1 = (s32[1,8]{1,0:T(1,128)}, s32[1,8]{1,0:T(1,128)S(1)}, u32[]{:S(2)}, u32[]{:S(2)}) collective-permute-start(s32[1,8]{1,0:T(1,128)} %param.9), channel_id=1, source_target_pairs={{0,8},{1,1},{2,18},{3,3},{4,12},{5,5},{6,22},{7,7},{8,0},{9,9},{10... | collective-permute-start | bytes 104 | tf_op jit(solution)/shard_map/ppermute | solution.py:226
  8.9 9.5 %collective-permute-start = (s32[1,8]{1,0:T(1,128)}, s32[1,8]{1,0:T(1,128)S(1)}, u32[]{:S(2)}, u32[]{:S(2)}) collective-permute-start(s32[1,8]{1,0:T(1,128)} %param.9), channel_id=1, source_target_pairs={{0,24},{1,493},{2,510},{3,503},{4,28},{5,489},{6,506},{7,499},{8,5... | collective-permute-start | bytes 104 | tf_op jit(solution)/shard_map/ppermute | solution.py:226
  18.8 9.2 %collective-permute-start.2 = (bf16[8,512]{1,0:T(8,128)(2,1)S(1)}, bf16[8,512]{1,0:T(8,128)(2,1)S(1)}, u32[]{:S(2)}, u32[]{:S(2)}) collective-permute-start(bf16[8,512]{1,0:T(8,128)(2,1)S(1)} %get-tuple-element.11), channel_id=1, source_target_pairs={{0,24},{1,493},{2,510},{3,503},{4,28},{5,489},{6,506},{7,499},{8,5... | collective-permute-start | bytes 24584 | tf_op jit(solution)/shard_map/ppermute | solution.py:235
  25.8 3.1 %collective-permute-start.3 = (bf16[8,512]{1,0:T(8,128)(2,1)S(1)}, bf16[8,512]{1,0:T(8,128)(2,1)S(1)}, u32[]{:S(2)}, u32[]{:S(2)}) collective-permute-start(bf16[8,512]{1,0:T(8,128)(2,1)S(1)} %get-tuple-element.12), channel_id=1, source_target_pairs={{0,8},{1,1},{2,18},{3,3},{4,12},{5,5},{6,22},{7,7},{8,0},{9,9},{10... | collective-permute-start | bytes 24584 | tf_op jit(solution)/shard_map/ppermute | solution.py:235
  29.5 7.9 %all-to-all-start = ((bf16[4,3,8,512]{3,2,1,0:T(8,128)(2,1)}), bf16[4,3,8,512]{3,2,1,0:T(8,128)(2,1)S(1)}, u32[]{:S(2)}, u32[]{:S(2)}) async-start(bf16[4,3,8,512]{3,2,1,0:T(8,128)(2,1)} %broadcast_in_dim.4), calls=%async_computation | async-start | bytes 196608 | tf_op jit(solution)/shard_map/all_to_all | solution.py:221
  39.7 32.5 %all-to-all-start.1 = ((bf16[4,784,128]{2,1,0:T(8,128)(2,1)}), bf16[4,784,128]{2,1,0:T(8,128)(2,1)S(1)}, u32[]{:S(2)}, u32[]{:S(2)}) async-start(bf16[4,784,128]{2,1,0:T(8,128)(2,1)} %broadcast_in_dim.5), calls=%async_computation.1 | async-start | bytes 1605632 | tf_op jit(solution)/shard_map/all_to_all | solution.py:221
  43.2 29.0 %collective-permute-start.4 = (bf16[784,128]{1,0:T(8,128)(2,1)S(1)}, bf16[784,128]{1,0:T(8,128)(2,1)S(1)}, u32[]{:S(2)}, u32[]{:S(2)}) collective-permute-start(bf16[784,128]{1,0:T(8,128)(2,1)S(1)} %contribution.1), channel_id=1, source_target_pairs={{0,4},{1,5},{2,6},{3,7},{4,0},{5,1},{6,2},{7,3},{8,12},{9,13},{10,... | collective-permute-start | bytes 602120 | tf_op jit(solution)/shard_map/ppermute | solution.py:251
  73.7 8.7 %all-to-all-start.2 = ((f32[4,32,128]{2,1,0:T(8,128)}), f32[4,32,128]{2,1,0:T(8,128)S(1)}, u32[]{:S(2)}, u32[]{:S(2)}) async-start(f32[4,32,128]{2,1,0:T(8,128)} %late.1), calls=%async_computation.2 | async-start | bytes 131072 | tf_op jit(solution)/shard_map/all_to_all | solution.py:278

commit v5 on v4

--- a/solution.py
+++ b/solution.py
@@ -14,7 +14,7 @@
 REACH = 3
 XN = 4
 DATA = OSUP * BF * NT * AB // 128
-ROWS = DATA + 16
+ROWS = DATA + 8
 F32 = jnp.float32
 BF16 = jnp.bfloat16
 
@@ -81,11 +81,11 @@
         sb_ref[pl.ds(2 * k + 1, OSUP // 2, stride=BF), :] = jnp.where(low8, s2, half)[: OSUP // 2]
     a_part = sa_ref[...].astype(BF16)
     b_part = sb_ref[...].astype(BF16)
-    lane = lax.broadcasted_iota(jnp.int32, (16, 128), 1)
+    lane = lax.broadcasted_iota(jnp.int32, (8, 128), 1)
     tag = jnp.where(lane == 0, a[0], jnp.where(lane == 1, a[1], a[2])).astype(F32).astype(BF16)
     out_ref[0:512, :] = a_part
     out_ref[512:768, :] = b_part
-    out_ref[768:784, :] = tag
+    out_ref[768:776, :] = tag
 
 
 def stage_kernel(*refs):
@@ -122,7 +122,7 @@
 
 
 def tags_of(block_ref, lead=()):
-    return blocks_of(block_ref[lead + (slice(768, 784), slice(None))][0:1])
+    return blocks_of(block_ref[lead + (slice(768, 776), slice(None))][0:1])
 
 
 def rows_of(columns_ref, rows, lanes):

time: 83.7 us -> 83.5 us (level)
  no operation moved by 1% of the time
where the time goes in v5:
time: 83.5 us; the launch traced here: 83 us
  starting transfers between devices  44 us (53%)
  waiting for transfers between devices  22.2 us (27%)
  Pallas kernels  14.2 us (17%)
  local copies, waits for them, and re-layouts  1.75 us (2%)
    ppermute x2, starting transfers between devices, per_device(): asked.append(lax.ppermute(support, axes, pairs[j]))  17 us
    ppermute x1, waiting for transfers between devices, per_device(): lax.ppermute(message, 'grp', [(g, (g + XN) % (2 * XN)) for g in range(2 *...  15 us
    ppermute x2, starting transfers between devices, per_device(): lax.ppermute(answer[j * OSUP:(j + 1) * OSUP], axes, pairs[j])  8.89 us
    ppermute x1, starting transfers between devices, per_device(): lax.ppermute(message, 'grp', [(g, (g + XN) % (2 * XN)) for g in range(2 *...  7.19 us
    all_to_all x2, starting transfers between devices, spread(): return lax.all_to_all(value, 'grp', 0, 0, axis_index_groups=groups)  6.8 us
    pallas_call x1, Pallas kernels, per_device(): pl.pallas_call(columns_kernel, out_shape=pltpu.VMEM((AUXR // AB, AB, XN *...  6.63 us
    all_to_all x1, starting transfers between devices, per_device(): late = lax.all_to_all(late, 'grp', 0, 0, axis_index_groups=groups)  4.18 us
    all_to_all x2, waiting for transfers between devices, spread(): return lax.all_to_all(value, 'grp', 0, 0, axis_index_groups=groups)  3.19 us
  transfers between devices with their start and end apart: 8, of which 5 were waited for; matrix products, arithmetic and copies ran while one was open for 0% of the time, Pallas kernels for 13%

profile of v5, /device:TPU:1, one launch (start us, length us, event | category | flops | bytes accessed | tf_op | source)
XLA Modules:
  0.0 83.0 jit_solution(18306580452482896235)
XLA Ops:
  0.0 8.9 %collective-permute-start.1 = (s32[1,8]{1,0:T(1,128)}, s32[1,8]{1,0:T(1,128)S(1)}, u32[]{:S(2)}, u32[]{:S(2)}) collective-permute-start(s32[1,8]{1,0:T(1,128)} %param.9), channel_id=1, source_target_pairs={{0,8},{1,1},{2,18},{3,3},{4,12},{5,5},{6,22},{7,7},{8,0},{9,9},{10... | collective-permute-start | bytes 104 | tf_op jit(solution)/shard_map/ppermute | solution.py:226
  8.9 8.1 %collective-permute-start = (s32[1,8]{1,0:T(1,128)}, s32[1,8]{1,0:T(1,128)S(1)}, u32[]{:S(2)}, u32[]{:S(2)}) collective-permute-start(s32[1,8]{1,0:T(1,128)} %param.9), channel_id=1, source_target_pairs={{0,24},{1,493},{2,510},{3,503},{4,28},{5,489},{6,506},{7,499},{8,5... | collective-permute-start | bytes 104 | tf_op jit(solution)/shard_map/ppermute | solution.py:226
  17.0 1.2 %shard_map.55 = bf16[512,1024]{1,0:T(8,128)(2,1)S(1)} custom-call(bf16[512,1024]{1,0:T(8,128)(2,1)} %refs_0_.2), custom_call_target="tpu_custom_call" | custom-call | tf_op jit(solution)/shard_map/pallas_call | solution.py:202
  18.3 0.1 collective-permute-done
  18.5 0.4 convolution_convert_fusion
  18.8 7.0 %collective-permute-start.2 = (bf16[8,512]{1,0:T(8,128)(2,1)S(1)}, bf16[8,512]{1,0:T(8,128)(2,1)S(1)}, u32[]{:S(2)}, u32[]{:S(2)}) collective-permute-start(bf16[8,512]{1,0:T(8,128)(2,1)S(1)} %get-tuple-element.11), channel_id=1, source_target_pairs={{0,24},{1,493},{2,510},{3,503},{4,28},{5,489},{6,506},{7,499},{8,5... | collective-permute-start | bytes 24584 | tf_op jit(solution)/shard_map/ppermute | solution.py:235
  25.8 1.9 %collective-permute-start.3 = (bf16[8,512]{1,0:T(8,128)(2,1)S(1)}, bf16[8,512]{1,0:T(8,128)(2,1)S(1)}, u32[]{:S(2)}, u32[]{:S(2)}) collective-permute-start(bf16[8,512]{1,0:T(8,128)(2,1)S(1)} %get-tuple-element.12), channel_id=1, source_target_pairs={{0,8},{1,1},{2,18},{3,3},{4,12},{5,5},{6,22},{7,7},{8,0},{9,9},{10... | collective-permute-start | bytes 24584 | tf_op jit(solution)/shard_map/ppermute | solution.py:235
  27.8 0.2 fusion.1
  28.0 0.8 %collective-permute-done.3 = bf16[8,512]{1,0:T(8,128)(2,1)S(1)} collective-permute-done((bf16[8,512]{1,0:T(8,128)(2,1)S(1)}, bf16[8,512]{1,0:T(8,128)(2,1)S(1)}, u32[]{:S(2)}, u32[]{:S(2)}) %collective-permute-start.3) | collective-permute-done | bytes 8224 | tf_op jit(solution)/shard_map/ppermute | solution.py:235
  28.9 0.7 broadcast_in_dim.4
  29.5 3.3 %all-to-all-start = ((bf16[4,3,8,512]{3,2,1,0:T(8,128)(2,1)}), bf16[4,3,8,512]{3,2,1,0:T(8,128)(2,1)S(1)}, u32[]{:S(2)}, u32[]{:S(2)}) async-start(bf16[4,3,8,512]{3,2,1,0:T(8,128)(2,1)} %broadcast_in_dim.4), calls=%async_computation | async-start | bytes 196608 | tf_op jit(solution)/shard_map/all_to_all | solution.py:221
  32.9 1.4 %shard_map.56.integrals_ref = bf16[1,1,3,64,4096]{4,3,2,1,0:T(8,128)(2,1)S(1)} custom-call(bf16[1,1,3,64,4096]{4,3,2,1,0:T(8,128)(2,1)} %refs_0_.3), custom_call_target="tpu_custom_call" | custom-call | tf_op jit(solution)/shard_map/pallas_call | solution.py:202
  34.3 3.2 %all-to-all-done.window_ref = bf16[4,3,8,512]{3,2,1,0:T(8,128)(2,1)S(1)} async-done(((bf16[4,3,8,512]{3,2,1,0:T(8,128)(2,1)}), bf16[4,3,8,512]{3,2,1,0:T(8,128)(2,1)S(1)}, u32[]{:S(2)}, u32[]{:S(2)}) %all-to-all-start) | async-done | bytes 98336 | tf_op jit(solution)/shard_map/all_to_all | solution.py:221
  37.5 1.2 %contribution.1 = bf16[776,128]{1,0:T(8,128)(2,1)S(1)} custom-call(s32[1]{0:T(128)} %bitcast.4.region_ref, s32[12]{0:T(128)S(1)} %reshape.17.pattern_ref, bf16[4,3,8,512]{3,2,1,0:T(8,128)(2,1)S(1)} %all-to-all-done.window_ref, bf16[1,1,3,64,4096]{4,3,2,1,0:T(8,128)(2,1)S(1)} %shard_map.56.integrals_ref), custom_call_target="tpu_custom_call" | custom-call | tf_op jit(solution)/shard_map/contribution/pallas_call | solution.py:241
  38.7 1.0 %broadcast_in_dim.5 = bf16[4,776,128]{2,1,0:T(8,128)(2,1)} broadcast(bf16[776,128]{1,0:T(8,128)(2,1)S(1)} %contribution.1), dimensions={1,2} | broadcast | bytes 993280 | tf_op jit(solution)/shard_map/broadcast_in_dim | solution.py:220
  39.7 3.5 %all-to-all-start.1 = ((bf16[4,776,128]{2,1,0:T(8,128)(2,1)}), bf16[4,776,128]{2,1,0:T(8,128)(2,1)S(1)}, u32[]{:S(2)}, u32[]{:S(2)}) async-start(bf16[4,776,128]{2,1,0:T(8,128)(2,1)} %broadcast_in_dim.5), calls=%async_computation.1 | async-start | bytes 1589248 | tf_op jit(solution)/shard_map/all_to_all | solution.py:221
  43.2 7.2 %collective-permute-start.4 = (bf16[776,128]{1,0:T(8,128)(2,1)S(1)}, bf16[776,128]{1,0:T(8,128)(2,1)S(1)}, u32[]{:S(2)}, u32[]{:S(2)}) collective-permute-start(bf16[776,128]{1,0:T(8,128)(2,1)S(1)} %contribution.1), channel_id=1, source_target_pairs={{0,4},{1,5},{2,6},{3,7},{4,0},{5,1},{6,2},{7,3},{8,12},{9,13},{10,... | collective-permute-start | bytes 595976 | tf_op jit(solution)/shard_map/ppermute | solution.py:251
  50.4 6.6 %columns.1.columns_ref = bf16[16,64,1024]{2,1,0:T(8,128)(2,1)S(1)} custom-call(bf16[4,3,8,512]{3,2,1,0:T(8,128)(2,1)S(1)} %all-to-all-done.window_ref, bf16[16,64,1024]{2,1,0:T(8,128)(2,1)} %bitcast.8), custom_call_target="tpu_custom_call" | custom-call | tf_op jit(solution)/shard_map/columns/pallas_call | solution.py:254
  57.0 15.0 %collective-permute-done.4.far_ref = bf16[776,128]{1,0:T(8,128)(2,1)S(1)} collective-permute-done((bf16[776,128]{1,0:T(8,128)(2,1)S(1)}, bf16[776,128]{1,0:T(8,128)(2,1)S(1)}, u32[]{:S(2)}, u32[]{:S(2)}) %collective-permute-start.4) | collective-permute-done | bytes 198688 | tf_op jit(solution)/shard_map/ppermute | solution.py:251
  72.0 1.5 %late.1 = f32[4,32,128]{2,1,0:T(8,128)} custom-call(bf16[776,128]{1,0:T(8,128)(2,1)S(1)} %collective-permute-done.4.far_ref, bf16[4,776,128]{2,1,0:T(8,128)(2,1)S(1)} %all-to-all-done.1.all_ref, bf16[16,64,1024]{2,1,0:T(8,128)(2,1)S(1)} %columns.1.columns_ref), custom_call_target="tpu_custom_call" | custom-call | tf_op jit(solution)/shard_map/late/pallas_call | solution.py:270
  73.6 4.2 %all-to-all-start.2 = ((f32[4,32,128]{2,1,0:T(8,128)}), f32[4,32,128]{2,1,0:T(8,128)S(1)}, u32[]{:S(2)}, u32[]{:S(2)}) async-start(f32[4,32,128]{2,1,0:T(8,128)} %late.1), calls=%async_computation.2 | async-start | bytes 131072 | tf_op jit(solution)/shard_map/all_to_all | solution.py:278
  77.7 1.4 %early.1.early_ref = f32[64,256]{1,0:T(8,128)S(1)} custom-call(s32[1]{0:T(128)} %bitcast.group_ref, bf16[4,776,128]{2,1,0:T(8,128)(2,1)S(1)} %all-to-all-done.1.all_ref, bf16[16,64,1024]{2,1,0:T(8,128)(2,1)S(1)} %columns.1.columns_ref), custom_call_target="tpu_custom_call" | custom-call | tf_op jit(solution)/shard_map/early/pallas_call | solution.py:262
  79.1 3.1 %all-to-all-done.2.late_ref = f32[4,32,128]{2,1,0:T(8,128)S(1)} async-done(((f32[4,32,128]{2,1,0:T(8,128)}), f32[4,32,128]{2,1,0:T(8,128)S(1)}, u32[]{:S(2)}, u32[]{:S(2)}) %all-to-all-start.2) | async-done | bytes 65568 | tf_op jit(solution)/shard_map/all_to_all | solution.py:278
  82.2 0.7 join.1
  (12 shorter events, 0.2 us)
Async XLA Ops:
  0.0 27.7 %copy-start = (s32[1,1,3,4]{3,1,2,0:T(1,128)S(1)}, s32[1,1,3,4]{3,1,2,0:T(1,128)}, u32[]{:S(2)}) copy-start(s32[1,1,3,4]{3,1,2,0:T(1,128)} %param.8) | copy-start | bytes 148
  0.0 18.3 %collective-permute-start.1 = (s32[1,8]{1,0:T(1,128)}, s32[1,8]{1,0:T(1,128)S(1)}, u32[]{:S(2)}, u32[]{:S(2)}) collective-permute-start(s32[1,8]{1,0:T(1,128)} %param.9), channel_id=1, source_target_pairs={{0,8},{1,1},{2,18},{3,3},{4,12},{5,5},{6,22},{7,7},{8,0},{9,9},{10... | collective-permute-start | bytes 104 | tf_op jit(solution)/shard_map/ppermute | solution.py:226
  8.9 9.5 %collective-permute-start = (s32[1,8]{1,0:T(1,128)}, s32[1,8]{1,0:T(1,128)S(1)}, u32[]{:S(2)}, u32[]{:S(2)}) collective-permute-start(s32[1,8]{1,0:T(1,128)} %param.9), channel_id=1, source_target_pairs={{0,24},{1,493},{2,510},{3,503},{4,28},{5,489},{6,506},{7,499},{8,5... | collective-permute-start | bytes 104 | tf_op jit(solution)/shard_map/ppermute | solution.py:226
  18.8 9.2 %collective-permute-start.2 = (bf16[8,512]{1,0:T(8,128)(2,1)S(1)}, bf16[8,512]{1,0:T(8,128)(2,1)S(1)}, u32[]{:S(2)}, u32[]{:S(2)}) collective-permute-start(bf16[8,512]{1,0:T(8,128)(2,1)S(1)} %get-tuple-element.11), channel_id=1, source_target_pairs={{0,24},{1,493},{2,510},{3,503},{4,28},{5,489},{6,506},{7,499},{8,5... | collective-permute-start | bytes 24584 | tf_op jit(solution)/shard_map/ppermute | solution.py:235
  25.8 3.1 %collective-permute-start.3 = (bf16[8,512]{1,0:T(8,128)(2,1)S(1)}, bf16[8,512]{1,0:T(8,128)(2,1)S(1)}, u32[]{:S(2)}, u32[]{:S(2)}) collective-permute-start(bf16[8,512]{1,0:T(8,128)(2,1)S(1)} %get-tuple-element.12), channel_id=1, source_target_pairs={{0,8},{1,1},{2,18},{3,3},{4,12},{5,5},{6,22},{7,7},{8,0},{9,9},{10... | collective-permute-start | bytes 24584 | tf_op jit(solution)/shard_map/ppermute | solution.py:235
  29.5 7.9 %all-to-all-start = ((bf16[4,3,8,512]{3,2,1,0:T(8,128)(2,1)}), bf16[4,3,8,512]{3,2,1,0:T(8,128)(2,1)S(1)}, u32[]{:S(2)}, u32[]{:S(2)}) async-start(bf16[4,3,8,512]{3,2,1,0:T(8,128)(2,1)} %broadcast_in_dim.4), calls=%async_computation | async-start | bytes 196608 | tf_op jit(solution)/shard_map/all_to_all | solution.py:221
  39.7 32.3 %all-to-all-start.1 = ((bf16[4,776,128]{2,1,0:T(8,128)(2,1)}), bf16[4,776,128]{2,1,0:T(8,128)(2,1)S(1)}, u32[]{:S(2)}, u32[]{:S(2)}) async-start(bf16[4,776,128]{2,1,0:T(8,128)(2,1)} %broadcast_in_dim.5), calls=%async_computation.1 | async-start | bytes 1589248 | tf_op jit(solution)/shard_map/all_to_all | solution.py:221
  43.2 28.8 %collective-permute-start.4 = (bf16[776,128]{1,0:T(8,128)(2,1)S(1)}, bf16[776,128]{1,0:T(8,128)(2,1)S(1)}, u32[]{:S(2)}, u32[]{:S(2)}) collective-permute-start(bf16[776,128]{1,0:T(8,128)(2,1)S(1)} %contribution.1), channel_id=1, source_target_pairs={{0,4},{1,5},{2,6},{3,7},{4,0},{5,1},{6,2},{7,3},{8,12},{9,13},{10,... | collective-permute-start | bytes 595976 | tf_op jit(solution)/shard_map/ppermute | solution.py:251
  73.6 8.7 %all-to-all-start.2 = ((f32[4,32,128]{2,1,0:T(8,128)}), f32[4,32,128]{2,1,0:T(8,128)S(1)}, u32[]{:S(2)}, u32[]{:S(2)}) async-start(f32[4,32,128]{2,1,0:T(8,128)} %late.1), calls=%async_computation.2 | async-start | bytes 131072 | tf_op jit(solution)/shard_map/all_to_all | solution.py:278

commit v6 on v5

--- a/solution.py
+++ b/solution.py
@@ -19,7 +19,7 @@
 BF16 = jnp.bfloat16
 
 
-TASKS = (((3, 0), (3, 1), (1, 1), (2, 1)), ((1, 0), (0, 0), (2, 0), (0, 0)))
+TASKS = (((3, 0), (3, 1), (1, 1), (2, 1)), ((2, 0), (0, 0), (0, 0), (1, 0)))
 
 
 def swap_pairs(j, regions, zlo):
@@ -48,8 +48,8 @@
         distance = jnp.abs(offset)
         place = jnp.where(distance == 2, region // 2, region) % 2
         phase = jnp.where(offset > 0, place, 1 - place)
-        x = jnp.where(distance == 3, phase, jnp.where(distance == 0, 1, 2 * phase))
-        x = jnp.where(distance == 2, 2 + phase, x)
+        x = jnp.where(distance == 3, phase, jnp.where(distance == 2, 3 * phase, 3 - phase))
+        x = jnp.where(distance == 0, 1, x)
         first = jnp.where(distance == 1, phase, jnp.where(distance == 2, phase, distance // 3))
         j = 1 - first
         m = pattern_ref[4 * t + 1]

time: 83.5 us -> 84.7 us (1.014)
  the two profiles are of different devices: /device:TPU:1 before, /device:TPU:24 now
where the time goes in v6:
time: 84.7 us; the launch traced here: 84.1 us
  starting transfers between devices  40 us (47%)
  waiting for transfers between devices  27.4 us (32%)
  Pallas kernels  14.2 us (17%)
  local copies, waits for them, and re-layouts  1.75 us (2%)
    ppermute x1, waiting for transfers between devices, per_device(): lax.ppermute(message, 'grp', [(g, (g + XN) % (2 * XN)) for g in range(2 *...  15.2 us
    all_to_all x2, starting transfers between devices, spread(): return lax.all_to_all(value, 'grp', 0, 0, axis_index_groups=groups)  14.5 us
    ppermute x1, starting transfers between devices, per_device(): lax.ppermute(message, 'grp', [(g, (g + XN) % (2 * XN)) for g in range(2 *...  8.35 us
    ppermute x2, starting transfers between devices, per_device(): lax.ppermute(answer[j * OSUP:(j + 1) * OSUP], axes, pairs[j])  6.82 us
    pallas_call x1, Pallas kernels, per_device(): pl.pallas_call(columns_kernel, out_shape=pltpu.VMEM((AUXR // AB, AB, XN *...  6.63 us
    ppermute x2, starting transfers between devices, per_device(): asked.append(lax.ppermute(support, axes, pairs[j]))  5.86 us
    all_to_all x2, waiting for transfers between devices, spread(): return lax.all_to_all(value, 'grp', 0, 0, axis_index_groups=groups)  4.76 us
    all_to_all x1, starting transfers between devices, per_device(): late = lax.all_to_all(late, 'grp', 0, 0, axis_index_groups=groups)  4.47 us
  transfers between devices with their start and end apart: 8, of which 5 were waited for; matrix products, arithmetic and copies ran while one was open for 0% of the time, Pallas kernels for 13%

profile of v6, /device:TPU:24, one launch (start us, length us, event | category | flops | bytes accessed | tf_op | source)
XLA Modules:
  0.0 84.1 jit_solution(9975535966810483663)
XLA Ops:
  0.0 3.9 %collective-permute-start.1 = (s32[1,8]{1,0:T(1,128)}, s32[1,8]{1,0:T(1,128)S(1)}, u32[]{:S(2)}, u32[]{:S(2)}) collective-permute-start(s32[1,8]{1,0:T(1,128)} %param.9), channel_id=1, source_target_pairs={{0,16},{1,1},{2,2},{3,11},{4,20},{5,5},{6,6},{7,15},{8,24},{9,9},{... | collective-permute-start | bytes 104 | tf_op jit(solution)/shard_map/ppermute | solution.py:226
  4.0 1.9 %collective-permute-start = (s32[1,8]{1,0:T(1,128)}, s32[1,8]{1,0:T(1,128)S(1)}, u32[]{:S(2)}, u32[]{:S(2)}) collective-permute-start(s32[1,8]{1,0:T(1,128)} %param.9), channel_id=1, source_target_pairs={{0,24},{1,493},{2,510},{3,503},{4,28},{5,489},{6,506},{7,499},{8,5... | collective-permute-start | bytes 104 | tf_op jit(solution)/shard_map/ppermute | solution.py:226
  5.9 1.2 %shard_map.55 = bf16[512,1024]{1,0:T(8,128)(2,1)S(1)} custom-call(bf16[512,1024]{1,0:T(8,128)(2,1)} %refs_0_.2), custom_call_target="tpu_custom_call" | custom-call | tf_op jit(solution)/shard_map/pallas_call | solution.py:202
  7.1 1.8 %collective-permute-done = s32[1,8]{1,0:T(1,128)S(1)} collective-permute-done((s32[1,8]{1,0:T(1,128)}, s32[1,8]{1,0:T(1,128)S(1)}, u32[]{:S(2)}, u32[]{:S(2)}) %collective-permute-start) | collective-permute-done | bytes 64 | tf_op jit(solution)/shard_map/ppermute | solution.py:226
  9.1 0.4 convolution_convert_fusion
  9.4 1.9 %collective-permute-start.2 = (bf16[8,512]{1,0:T(8,128)(2,1)S(1)}, bf16[8,512]{1,0:T(8,128)(2,1)S(1)}, u32[]{:S(2)}, u32[]{:S(2)}) collective-permute-start(bf16[8,512]{1,0:T(8,128)(2,1)S(1)} %get-tuple-element.11), channel_id=1, source_target_pairs={{0,24},{1,493},{2,510},{3,503},{4,28},{5,489},{6,506},{7,499},{8,5... | collective-permute-start | bytes 24584 | tf_op jit(solution)/shard_map/ppermute | solution.py:235
  11.4 4.9 %collective-permute-start.3 = (bf16[8,512]{1,0:T(8,128)(2,1)S(1)}, bf16[8,512]{1,0:T(8,128)(2,1)S(1)}, u32[]{:S(2)}, u32[]{:S(2)}) collective-permute-start(bf16[8,512]{1,0:T(8,128)(2,1)S(1)} %get-tuple-element.12), channel_id=1, source_target_pairs={{0,16},{1,1},{2,2},{3,11},{4,20},{5,5},{6,6},{7,15},{8,24},{9,9},{... | collective-permute-start | bytes 24584 | tf_op jit(solution)/shard_map/ppermute | solution.py:235
  16.3 0.2 fusion.1
  16.6 1.3 %collective-permute-done.3 = bf16[8,512]{1,0:T(8,128)(2,1)S(1)} collective-permute-done((bf16[8,512]{1,0:T(8,128)(2,1)S(1)}, bf16[8,512]{1,0:T(8,128)(2,1)S(1)}, u32[]{:S(2)}, u32[]{:S(2)}) %collective-permute-start.3) | collective-permute-done | bytes 8224 | tf_op jit(solution)/shard_map/ppermute | solution.py:235
  17.9 0.7 broadcast_in_dim.4
  18.5 11.0 %all-to-all-start = ((bf16[4,3,8,512]{3,2,1,0:T(8,128)(2,1)}), bf16[4,3,8,512]{3,2,1,0:T(8,128)(2,1)S(1)}, u32[]{:S(2)}, u32[]{:S(2)}) async-start(bf16[4,3,8,512]{3,2,1,0:T(8,128)(2,1)} %broadcast_in_dim.4), calls=%async_computation | async-start | bytes 196608 | tf_op jit(solution)/shard_map/all_to_all | solution.py:221
  29.6 1.4 %shard_map.56.integrals_ref = bf16[1,1,3,64,4096]{4,3,2,1,0:T(8,128)(2,1)S(1)} custom-call(bf16[1,1,3,64,4096]{4,3,2,1,0:T(8,128)(2,1)} %refs_0_.3), custom_call_target="tpu_custom_call" | custom-call | tf_op jit(solution)/shard_map/pallas_call | solution.py:202
  31.0 4.8 %all-to-all-done.window_ref = bf16[4,3,8,512]{3,2,1,0:T(8,128)(2,1)S(1)} async-done(((bf16[4,3,8,512]{3,2,1,0:T(8,128)(2,1)}), bf16[4,3,8,512]{3,2,1,0:T(8,128)(2,1)S(1)}, u32[]{:S(2)}, u32[]{:S(2)}) %all-to-all-start) | async-done | bytes 98336 | tf_op jit(solution)/shard_map/all_to_all | solution.py:221
  35.7 1.2 %contribution.1 = bf16[776,128]{1,0:T(8,128)(2,1)S(1)} custom-call(s32[1]{0:T(128)} %bitcast.4.region_ref, s32[12]{0:T(128)S(1)} %reshape.17.pattern_ref, bf16[4,3,8,512]{3,2,1,0:T(8,128)(2,1)S(1)} %all-to-all-done.window_ref, bf16[1,1,3,64,4096]{4,3,2,1,0:T(8,128)(2,1)S(1)} %shard_map.56.integrals_ref), custom_call_target="tpu_custom_call" | custom-call | tf_op jit(solution)/shard_map/contribution/pallas_call | solution.py:241
  37.0 1.0 %broadcast_in_dim.5 = bf16[4,776,128]{2,1,0:T(8,128)(2,1)} broadcast(bf16[776,128]{1,0:T(8,128)(2,1)S(1)} %contribution.1), dimensions={1,2} | broadcast | bytes 993280 | tf_op jit(solution)/shard_map/broadcast_in_dim | solution.py:220
  38.0 3.5 %all-to-all-start.1 = ((bf16[4,776,128]{2,1,0:T(8,128)(2,1)}), bf16[4,776,128]{2,1,0:T(8,128)(2,1)S(1)}, u32[]{:S(2)}, u32[]{:S(2)}) async-start(bf16[4,776,128]{2,1,0:T(8,128)(2,1)} %broadcast_in_dim.5), calls=%async_computation.1 | async-start | bytes 1589248 | tf_op jit(solution)/shard_map/all_to_all | solution.py:221
  41.5 8.3 %collective-permute-start.4 = (bf16[776,128]{1,0:T(8,128)(2,1)S(1)}, bf16[776,128]{1,0:T(8,128)(2,1)S(1)}, u32[]{:S(2)}, u32[]{:S(2)}) collective-permute-start(bf16[776,128]{1,0:T(8,128)(2,1)S(1)} %contribution.1), channel_id=1, source_target_pairs={{0,4},{1,5},{2,6},{3,7},{4,0},{5,1},{6,2},{7,3},{8,12},{9,13},{10,... | collective-permute-start | bytes 595976 | tf_op jit(solution)/shard_map/ppermute | solution.py:251
  49.8 6.6 %columns.1.columns_ref = bf16[16,64,1024]{2,1,0:T(8,128)(2,1)S(1)} custom-call(bf16[4,3,8,512]{3,2,1,0:T(8,128)(2,1)S(1)} %all-to-all-done.window_ref, bf16[16,64,1024]{2,1,0:T(8,128)(2,1)} %bitcast.8), custom_call_target="tpu_custom_call" | custom-call | tf_op jit(solution)/shard_map/columns/pallas_call | solution.py:254
  56.5 15.2 %collective-permute-done.4.far_ref = bf16[776,128]{1,0:T(8,128)(2,1)S(1)} collective-permute-done((bf16[776,128]{1,0:T(8,128)(2,1)S(1)}, bf16[776,128]{1,0:T(8,128)(2,1)S(1)}, u32[]{:S(2)}, u32[]{:S(2)}) %collective-permute-start.4) | collective-permute-done | bytes 198688 | tf_op jit(solution)/shard_map/ppermute | solution.py:251
  71.7 1.5 %late.1 = f32[4,32,128]{2,1,0:T(8,128)} custom-call(bf16[776,128]{1,0:T(8,128)(2,1)S(1)} %collective-permute-done.4.far_ref, bf16[4,776,128]{2,1,0:T(8,128)(2,1)S(1)} %all-to-all-done.1.all_ref, bf16[16,64,1024]{2,1,0:T(8,128)(2,1)S(1)} %columns.1.columns_ref), custom_call_target="tpu_custom_call" | custom-call | tf_op jit(solution)/shard_map/late/pallas_call | solution.py:270
  73.2 4.5 %all-to-all-start.2 = ((f32[4,32,128]{2,1,0:T(8,128)}), f32[4,32,128]{2,1,0:T(8,128)S(1)}, u32[]{:S(2)}, u32[]{:S(2)}) async-start(f32[4,32,128]{2,1,0:T(8,128)} %late.1), calls=%async_computation.2 | async-start | bytes 131072 | tf_op jit(solution)/shard_map/all_to_all | solution.py:278
  77.7 1.4 %early.1.early_ref = f32[64,256]{1,0:T(8,128)S(1)} custom-call(s32[1]{0:T(128)} %bitcast.group_ref, bf16[4,776,128]{2,1,0:T(8,128)(2,1)S(1)} %all-to-all-done.1.all_ref, bf16[16,64,1024]{2,1,0:T(8,128)(2,1)S(1)} %columns.1.columns_ref), custom_call_target="tpu_custom_call" | custom-call | tf_op jit(solution)/shard_map/early/pallas_call | solution.py:262
  79.1 4.2 %all-to-all-done.2.late_ref = f32[4,32,128]{2,1,0:T(8,128)S(1)} async-done(((f32[4,32,128]{2,1,0:T(8,128)}), f32[4,32,128]{2,1,0:T(8,128)S(1)}, u32[]{:S(2)}, u32[]{:S(2)}) %all-to-all-start.2) | async-done | bytes 65568 | tf_op jit(solution)/shard_map/all_to_all | solution.py:278
  83.3 0.7 join.1
  (12 shorter events, 0.2 us)
Async XLA Ops:
  0.0 16.3 %copy-start = (s32[1,1,3,4]{3,1,2,0:T(1,128)S(1)}, s32[1,1,3,4]{3,1,2,0:T(1,128)}, u32[]{:S(2)}) copy-start(s32[1,1,3,4]{3,1,2,0:T(1,128)} %param.8) | copy-start | bytes 148
  0.0 7.1 %collective-permute-start.1 = (s32[1,8]{1,0:T(1,128)}, s32[1,8]{1,0:T(1,128)S(1)}, u32[]{:S(2)}, u32[]{:S(2)}) collective-permute-start(s32[1,8]{1,0:T(1,128)} %param.9), channel_id=1, source_target_pairs={{0,16},{1,1},{2,2},{3,11},{4,20},{5,5},{6,6},{7,15},{8,24},{9,9},{... | collective-permute-start | bytes 104 | tf_op jit(solution)/shard_map/ppermute | solution.py:226
  4.0 5.0 %collective-permute-start = (s32[1,8]{1,0:T(1,128)}, s32[1,8]{1,0:T(1,128)S(1)}, u32[]{:S(2)}, u32[]{:S(2)}) collective-permute-start(s32[1,8]{1,0:T(1,128)} %param.9), channel_id=1, source_target_pairs={{0,24},{1,493},{2,510},{3,503},{4,28},{5,489},{6,506},{7,499},{8,5... | collective-permute-start | bytes 104 | tf_op jit(solution)/shard_map/ppermute | solution.py:226
  9.4 7.1 %collective-permute-start.2 = (bf16[8,512]{1,0:T(8,128)(2,1)S(1)}, bf16[8,512]{1,0:T(8,128)(2,1)S(1)}, u32[]{:S(2)}, u32[]{:S(2)}) collective-permute-start(bf16[8,512]{1,0:T(8,128)(2,1)S(1)} %get-tuple-element.11), channel_id=1, source_target_pairs={{0,24},{1,493},{2,510},{3,503},{4,28},{5,489},{6,506},{7,499},{8,5... | collective-permute-start | bytes 24584 | tf_op jit(solution)/shard_map/ppermute | solution.py:235
  11.4 6.5 %collective-permute-start.3 = (bf16[8,512]{1,0:T(8,128)(2,1)S(1)}, bf16[8,512]{1,0:T(8,128)(2,1)S(1)}, u32[]{:S(2)}, u32[]{:S(2)}) collective-permute-start(bf16[8,512]{1,0:T(8,128)(2,1)S(1)} %get-tuple-element.12), channel_id=1, source_target_pairs={{0,16},{1,1},{2,2},{3,11},{4,20},{5,5},{6,6},{7,15},{8,24},{9,9},{... | collective-permute-start | bytes 24584 | tf_op jit(solution)/shard_map/ppermute | solution.py:235
  18.5 17.2 %all-to-all-start = ((bf16[4,3,8,512]{3,2,1,0:T(8,128)(2,1)}), bf16[4,3,8,512]{3,2,1,0:T(8,128)(2,1)S(1)}, u32[]{:S(2)}, u32[]{:S(2)}) async-start(bf16[4,3,8,512]{3,2,1,0:T(8,128)(2,1)} %broadcast_in_dim.4), calls=%async_computation | async-start | bytes 196608 | tf_op jit(solution)/shard_map/all_to_all | solution.py:221
  38.0 33.7 %all-to-all-start.1 = ((bf16[4,776,128]{2,1,0:T(8,128)(2,1)}), bf16[4,776,128]{2,1,0:T(8,128)(2,1)S(1)}, u32[]{:S(2)}, u32[]{:S(2)}) async-start(bf16[4,776,128]{2,1,0:T(8,128)(2,1)} %broadcast_in_dim.5), calls=%async_computation.1 | async-start | bytes 1589248 | tf_op jit(solution)/shard_map/all_to_all | solution.py:221
  41.5 30.2 %collective-permute-start.4 = (bf16[776,128]{1,0:T(8,128)(2,1)S(1)}, bf16[776,128]{1,0:T(8,128)(2,1)S(1)}, u32[]{:S(2)}, u32[]{:S(2)}) collective-permute-start(bf16[776,128]{1,0:T(8,128)(2,1)S(1)} %contribution.1), channel_id=1, source_target_pairs={{0,4},{1,5},{2,6},{3,7},{4,0},{5,1},{6,2},{7,3},{8,12},{9,13},{10,... | collective-permute-start | bytes 595976 | tf_op jit(solution)/shard_map/ppermute | solution.py:251
  73.2 10.1 %all-to-all-start.2 = ((f32[4,32,128]{2,1,0:T(8,128)}), f32[4,32,128]{2,1,0:T(8,128)S(1)}, u32[]{:S(2)}, u32[]{:S(2)}) async-start(f32[4,32,128]{2,1,0:T(8,128)} %late.1), calls=%async_computation.2 | async-start | bytes 131072 | tf_op jit(solution)/shard_map/all_to_all | solution.py:278
